TPU v7x, 32 devices: a whole 2x2x4 slice. The times are simulated.
32 devices in a mesh: blk: 8 (over z, y), layer: 4 (over x, core).
Axes of the slice: x: 2, y: 2, z: 4, core: 2. Of those that a mesh axis runs over, the one named last changes fastest.
Arguments:
- source: float32 [64, 512, 128], P('layer', 'blk'), may hold values from -18 to 18
- sigma_ref: float32 [64, 512, 128], P('layer', 'blk'), may hold values from 0.3 to 3
- owner: int32 [64, 512], P('layer', 'blk'), may hold values from 0 to 31, as said below
- slot: int32 [64, 512], P('layer', 'blk'), may hold values from 0 to 1023, as said below
- temp_old: float32 [32768, 128], P(('blk', 'layer')), may hold values from 0 to 2
- heat_cap: float32 [32768, 128], P(('blk', 'layer')), may hold values from 0.5 to 4
- conduct: float32 [32768, 128], P(('blk', 'layer')), may hold values from 0.2 to 2
Outputs:
- potential: float32 [64, 512, 128], P('layer', 'blk')
- temp_new: float32 [32768, 128], P(('blk', 'layer'))
Inputs may be any that keep to these rules, and one draw needn't show every extreme that they name: Among the 1024 blocks of one electric subdomain, at most 64 name the same owner, and 64 is reached in every subdomain. The pairs (owner, slot) are all different: every owner receives exactly 1024 blocks, one for each of its rows.
All inputs are finite; a program needn't handle non-finite values.
Results may differ from a plain program's by a relative error of at most 0.00002.
Values sent between devices are 32-bit elements; how exact they have to be, the bound alone decides.
A program may use at most 64 MiB of HBM per device.

v0:
```python
import jax
import jax.numpy as jnp
from jax import lax
from jax.sharding import PartitionSpec as P

SWEEPS = 3
JACOBI = 2


COUPLE = 0.4
THETA = 1.125
DELTA = 0.875


def with_halo(cells, sides, width, closed):
    for axis, dim in sides:
        count = lax.axis_size(axis)
        ends = count if closed else count - 1
        head = lax.slice_in_dim(cells, 0, width, axis=dim)
        tail = lax.slice_in_dim(cells, cells.shape[dim] - width, cells.shape[dim], axis=dim)
        cells = jnp.concatenate(
            [
                lax.ppermute(tail, axis, [(i, (i + 1) % count) for i in range(ends)]),
                cells,
                lax.ppermute(head, axis, [((i + 1) % count, i) for i in range(ends)]),
            ],
            axis=dim,
        )
    return cells


def neighbours(field):
    slab_pad = with_halo(field, (("layer", 0),), 1, False)
    cycle_pad = with_halo(field, (("blk", 1),), 1, True)
    radial = jnp.pad(field, ((0, 0), (0, 0), (1, 1)))
    return [
        slab_pad[2:],
        slab_pad[:-2],
        cycle_pad[:, 2:],
        cycle_pad[:, :-2],
        radial[:, :, 2:],
        radial[:, :, :-2],
    ]


def electric(source, cond_here):
    couplings = [0.5 * (cond_here + other) for other in neighbours(cond_here)]
    diag_sum = couplings[0]
    for coupling in couplings[1:]:
        diag_sum = diag_sum + coupling
    inv_diag = 1.0 / diag_sum
    ratio = THETA / DELTA
    potential = jnp.zeros_like(source)
    residual = source
    search_dir = inv_diag * residual / THETA
    rho_now = 1.0 / ratio
    for sweep in range(SWEEPS):
        potential = potential + search_dir
        if sweep + 1 < SWEEPS:
            result = jnp.zeros_like(search_dir)
            for operate_coupling, operate_other in zip(couplings, neighbours(search_dir)):
                result = result + operate_coupling * (search_dir - operate_other)
            residual = residual - result
            rho_next = 1.0 / (2.0 * ratio - rho_now)
            search_dir = rho_next * rho_now * search_dir + 2.0 * rho_next / DELTA * (
                inv_diag * residual
            )
            rho_now = rho_next
    return potential


def joule(potential, cond_here):
    result = jnp.zeros_like(potential)
    for other in neighbours(potential):
        gap = potential - other
        result = result + 0.5 * gap * gap
    return cond_here * result


def thermal_step(temp_old, heat_cap, conduct, heat):
    faces = 0.5 * (conduct[:, 1:] + conduct[:, :-1])
    edge = jnp.zeros((conduct.shape[0], 1), jnp.float32)
    left_cond = jnp.concatenate([edge, faces], axis=1)
    right_cond = jnp.concatenate([faces, edge], axis=1)
    diag_sum = heat_cap + left_cond + right_cond
    target = heat_cap * temp_old + heat
    current = temp_old
    for sweep in range(JACOBI):
        before = jnp.concatenate([edge, current[:, :-1]], axis=1)
        after = jnp.concatenate([current[:, 1:], edge], axis=1)
        current = (target + left_cond * before + right_cond * after) / diag_sum
    return current


def send_places(owner, peers):
    owners = owner.reshape(-1)
    block_count = owners.shape[0]
    capacity = 2 * block_count // peers
    ordering = jnp.argsort(owners, stable=True)
    ranked = owners[ordering]
    run_start = jnp.searchsorted(ranked, ranked, side="left")
    placed = jnp.arange(block_count, dtype=jnp.int32) - run_start
    within = jnp.zeros((block_count,), jnp.int32).at[ordering].set(placed)
    return (owners * capacity + within, capacity)


def per_device(source, sigma_ref, owner, slot, temp_old, heat_cap, conduct):
    peers = lax.axis_size(("blk", "layer"))
    radial = source.shape[2]
    block_count = temp_old.shape[0]
    positions, capacity = send_places(owner, peers)
    outgoing_slots = (
        jnp.full((peers * capacity,), block_count, jnp.int32).at[positions].set(slot.reshape(-1))
    )
    wanted = lax.all_to_all(
        outgoing_slots.reshape(peers, capacity),
        ("blk", "layer"),
        split_axis=0,
        concat_axis=0,
        tiled=True,
    ).reshape(-1)
    replies = jnp.take(temp_old, wanted, axis=0, mode="fill", fill_value=0.0).reshape(
        peers, capacity, radial
    )
    fetched = lax.all_to_all(replies, ("blk", "layer"), split_axis=0, concat_axis=0, tiled=True)
    temp_here = jnp.take(fetched.reshape(-1, radial), positions, axis=0).reshape(source.shape)
    cond_here = sigma_ref / (1.0 + COUPLE * temp_here)
    potential = electric(source, cond_here)
    power = joule(potential, cond_here)
    total = lax.psum(jnp.sum(power), ("blk", "layer"))
    factor = source.size * peers / total
    power = power * factor
    outgoing = (
        jnp.zeros((peers * capacity, radial), jnp.float32)
        .at[positions]
        .set(power.reshape(-1, radial))
    )
    arrived = lax.all_to_all(
        outgoing.reshape(peers, capacity, radial),
        ("blk", "layer"),
        split_axis=0,
        concat_axis=0,
        tiled=True,
    )
    arrived = arrived.reshape(-1, radial)
    heat = jnp.zeros((block_count, radial), jnp.float32).at[wanted].set(arrived, mode="drop")
    temp_new = thermal_step(temp_old, heat_cap, conduct, heat)
    return (potential, temp_new)


def solution(mesh):
    return jax.shard_map(
        per_device,
        mesh=mesh,
        in_specs=(
            P("layer", "blk", None),
            P("layer", "blk", None),
            P("layer", "blk"),
            P("layer", "blk"),
            P(("blk", "layer"), None),
            P(("blk", "layer"), None),
            P(("blk", "layer"), None),
        ),
        out_specs=(P("layer", "blk", None), P(("blk", "layer"), None)),
        check_vma=False,
    )
```

profile of v0, /device:TPU:1, one launch (start us, length us, event | category | flops | bytes accessed | tf_op | source)
XLA Modules:
  0.0 254.6 jit_solution(13507090287348213047)
XLA Ops:
  1.4 4.4 %sort.17 = (s32[1024]{0:T(1024)}, s32[1024]{0:T(1024)S(1)}) sort(s32[1024]{0:T(1024)S(1)} %reshape.86, s32[1024]{0:T(1024)S(1)} %iota.7), dimensions={0}, to_apply=%region_0.0 | sort | flops 10240 | bytes 16384 | tf_op jit(solution)/shard_map/jit(argsort)/sort | solution.py:99
  5.8 4.5 %gather_fusion.1 = s32[1024]{0:T(1024)S(1)} fusion(s32[1024]{0:T(1024)S(1)} %reshape.86, s32[1024]{0:T(1024)S(1)} %get-tuple-element.125), kind=kCustom, calls=%fused_computation.1 | custom fusion | bytes 12288 | tf_op jit(solution)/shard_map/gather | solution.py:100
  10.3 50.7 %while.25 = (s32[]{:T(128)}, u32[1024]{0:T(1024)S(1)}, u32[1024]{0:T(1024)S(1)}, s32[1024]{0:T(1024)S(1)}, s32[]{:T(128)}, /*index=5*/s32[]{:T(128)}, s32[]{}) while((s32[]{:T(128)}, u32[1024]{0:T(1024)S(1)}, u32[1024]{0:T(1024)S(1)}, s32[1024]{0:T(1024)S(1)}, s32[]{:T(128)}, /*index=5*/s32[]{:T(128)}, s32[]{}) %tuple.55), condition=%wide.region_2.3_spmd.clone, body=%wide.region_1.2_spmd.clone.sunk | while | flops 19460 | bytes 67685 | solution.py:101
  10.4 4.5 %gather_fusion = s32[1024]{0:T(1024)S(1)} fusion(s32[1024]{0:T(1024)S(1)} %get-tuple-element.173, u32[1024]{0:T(1024)S(1)} %broadcast_clamp_fusion.5), kind=kCustom, calls=%fused_computation.clone.clone.1 | custom fusion | bytes 12288 | tf_op jit(solution)/shard_map/jit(searchsorted)/jit(_searchsorted_scan_impl)/vmap(jit(_searchsorted_scan_impl))/while/body/eval_jaxpr/gather | solution.py:101
  15.0 4.5 %gather_fusion = s32[1024]{0:T(1024)S(1)} fusion(s32[1024]{0:T(1024)S(1)} %get-tuple-element.173, u32[1024]{0:T(1024)S(1)} %broadcast_clamp_fusion.5), kind=kCustom, calls=%fused_computation.clone.clone.1 | custom fusion | bytes 12288 | tf_op jit(solution)/shard_map/jit(searchsorted)/jit(_searchsorted_scan_impl)/vmap(jit(_searchsorted_scan_impl))/while/body/eval_jaxpr/gather | solution.py:101
  19.6 4.5 %gather_fusion = s32[1024]{0:T(1024)S(1)} fusion(s32[1024]{0:T(1024)S(1)} %get-tuple-element.173, u32[1024]{0:T(1024)S(1)} %broadcast_clamp_fusion.5), kind=kCustom, calls=%fused_computation.clone.clone.1 | custom fusion | bytes 12288 | tf_op jit(solution)/shard_map/jit(searchsorted)/jit(_searchsorted_scan_impl)/vmap(jit(_searchsorted_scan_impl))/while/body/eval_jaxpr/gather | solution.py:101
  24.2 4.5 %gather_fusion = s32[1024]{0:T(1024)S(1)} fusion(s32[1024]{0:T(1024)S(1)} %get-tuple-element.173, u32[1024]{0:T(1024)S(1)} %broadcast_clamp_fusion.5), kind=kCustom, calls=%fused_computation.clone.clone.1 | custom fusion | bytes 12288 | tf_op jit(solution)/shard_map/jit(searchsorted)/jit(_searchsorted_scan_impl)/vmap(jit(_searchsorted_scan_impl))/while/body/eval_jaxpr/gather | solution.py:101
  28.8 4.5 %gather_fusion = s32[1024]{0:T(1024)S(1)} fusion(s32[1024]{0:T(1024)S(1)} %get-tuple-element.173, u32[1024]{0:T(1024)S(1)} %broadcast_clamp_fusion.5), kind=kCustom, calls=%fused_computation.clone.clone.1 | custom fusion | bytes 12288 | tf_op jit(solution)/shard_map/jit(searchsorted)/jit(_searchsorted_scan_impl)/vmap(jit(_searchsorted_scan_impl))/while/body/eval_jaxpr/gather | solution.py:101
  33.4 4.5 %gather_fusion = s32[1024]{0:T(1024)S(1)} fusion(s32[1024]{0:T(1024)S(1)} %get-tuple-element.173, u32[1024]{0:T(1024)S(1)} %broadcast_clamp_fusion.5), kind=kCustom, calls=%fused_computation.clone.clone.1 | custom fusion | bytes 12288 | tf_op jit(solution)/shard_map/jit(searchsorted)/jit(_searchsorted_scan_impl)/vmap(jit(_searchsorted_scan_impl))/while/body/eval_jaxpr/gather | solution.py:101
  38.0 4.5 %gather_fusion = s32[1024]{0:T(1024)S(1)} fusion(s32[1024]{0:T(1024)S(1)} %get-tuple-element.173, u32[1024]{0:T(1024)S(1)} %broadcast_clamp_fusion.5), kind=kCustom, calls=%fused_computation.clone.clone.1 | custom fusion | bytes 12288 | tf_op jit(solution)/shard_map/jit(searchsorted)/jit(_searchsorted_scan_impl)/vmap(jit(_searchsorted_scan_impl))/while/body/eval_jaxpr/gather | solution.py:101
  42.6 4.5 %gather_fusion = s32[1024]{0:T(1024)S(1)} fusion(s32[1024]{0:T(1024)S(1)} %get-tuple-element.173, u32[1024]{0:T(1024)S(1)} %broadcast_clamp_fusion.5), kind=kCustom, calls=%fused_computation.clone.clone.1 | custom fusion | bytes 12288 | tf_op jit(solution)/shard_map/jit(searchsorted)/jit(_searchsorted_scan_impl)/vmap(jit(_searchsorted_scan_impl))/while/body/eval_jaxpr/gather | solution.py:101
  47.3 4.5 %gather_fusion = s32[1024]{0:T(1024)S(1)} fusion(s32[1024]{0:T(1024)S(1)} %get-tuple-element.173, u32[1024]{0:T(1024)S(1)} %broadcast_clamp_fusion.5), kind=kCustom, calls=%fused_computation.clone.clone.1 | custom fusion | bytes 12288 | tf_op jit(solution)/shard_map/jit(searchsorted)/jit(_searchsorted_scan_impl)/vmap(jit(_searchsorted_scan_impl))/while/body/eval_jaxpr/gather | solution.py:101
  51.9 4.5 %gather_fusion = s32[1024]{0:T(1024)S(1)} fusion(s32[1024]{0:T(1024)S(1)} %get-tuple-element.173, u32[1024]{0:T(1024)S(1)} %broadcast_clamp_fusion.5), kind=kCustom, calls=%fused_computation.clone.clone.1 | custom fusion | bytes 12288 | tf_op jit(solution)/shard_map/jit(searchsorted)/jit(_searchsorted_scan_impl)/vmap(jit(_searchsorted_scan_impl))/while/body/eval_jaxpr/gather | solution.py:101
  56.5 4.5 %gather_fusion = s32[1024]{0:T(1024)S(1)} fusion(s32[1024]{0:T(1024)S(1)} %get-tuple-element.173, u32[1024]{0:T(1024)S(1)} %broadcast_clamp_fusion.5), kind=kCustom, calls=%fused_computation.clone.clone.1 | custom fusion | bytes 12288 | tf_op jit(solution)/shard_map/jit(searchsorted)/jit(_searchsorted_scan_impl)/vmap(jit(_searchsorted_scan_impl))/while/body/eval_jaxpr/gather | solution.py:101
  61.1 4.3 %scatter_custom_fusion = s32[1024]{0:T(1024)S(1)} fusion(s32[1024]{0:T(1024)S(1)} %get-tuple-element.126, s32[1024]{0:T(1024)S(1)} %convert_subtract_fusion, s32[]{:T(128)} %constant.81.clone.1), kind=kCustom, calls=%fused_computation.133 | custom fusion | bytes 4100 | tf_op jit(solution)/shard_map/scatter | solution.py:103
  65.5 4.3 %scatter_custom_fusion.1 = s32[2048]{0:T(1024)S(1)} fusion(s32[1024]{0:T(1024)S(1)} %get-tuple-element.104, s32[1024]{0:T(1024)S(1)} %reshape.138, s32[]{:T(128)} %constant.82.clone.1), kind=kCustom, calls=%fused_computation.127 | custom fusion | bytes 8196 | tf_op jit(solution)/shard_map/scatter | solution.py:113
  69.9 13.7 %all_to_all.19 = s32[32,1,64]{2,1,0:T(1,128)S(1)} all-to-all(s32[32,1,64]{2,1,0:T(1,128)S(1)} %all_to_all.12), channel_id=1, replica_groups=mesh['blk'=8,'layer'=4] {'blk','layer'}, dimensions={0} | all-to-all | bytes 16384 | tf_op jit(solution)/shard_map/all_to_all | solution.py:115
  84.9 5.5 %gather_fusion.2 = f32[2048,128]{1,0:T(8,128)S(1)} fusion(f32[1024,128]{1,0:T(8,128)S(1)} %copy-done, s32[2048]{0:T(1024)S(1)} %broadcast_clamp_fusion.1), kind=kCustom, calls=%fused_computation.2 | custom fusion | bytes 2105344 | tf_op jit(solution)/shard_map/jit(_take)/gather | solution.py:122
  94.7 25.4 %all-to-all-done.1 = f32[32,64,128]{2,1,0:T(8,128)S(1)} async-done(((f32[32,64,128]{2,1,0:T(8,128)}), f32[32,64,128]{2,1,0:T(8,128)S(1)}, u32[]{:S(2)}, u32[]{:S(2)}) %all-to-all-start.1) | async-done | bytes 1048608 | tf_op jit(solution)/shard_map/all_to_all | solution.py:125
  132.3 4.7 %collective-permute-done.3 = f32[16,1,128]{2,1,0:T(1,128)S(1)} collective-permute-done((f32[16,1,128]{2,1,0:T(1,128)S(1)}, f32[16,1,128]{2,1,0:T(1,128)S(1)}, u32[]{:S(2)}, u32[]{:S(2)}) %collective-permute-start.3) | collective-permute-done | bytes 8224 | tf_op jit(solution)/shard_map/ppermute | solution.py:23
  173.2 36.0 %psum.7 = f32[]{:T(128)} all-reduce(f32[]{:T(128)} %get-tuple-element.97), channel_id=1, replica_groups=mesh['blk'=8,'layer'=4] {'blk','layer'}, use_global_device_ids=true, to_apply=%region_6.7 | all-reduce | flops 1 | bytes 8 | tf_op jit(solution)/shard_map/psum | solution.py:130
  214.0 7.3 %all-to-all-start.2 = ((f32[32,64,128]{2,1,0:T(8,128)}), f32[32,64,128]{2,1,0:T(8,128)}, u32[]{:S(2)}, u32[]{:S(2)}) async-start(f32[32,64,128]{2,1,0:T(8,128)} %bitcast.6), calls=%async_computation.2 | async-start | bytes 2097152 | tf_op jit(solution)/shard_map/all_to_all | solution.py:138
  221.8 24.9 %all-to-all-done.2 = f32[32,64,128]{2,1,0:T(8,128)} async-done(((f32[32,64,128]{2,1,0:T(8,128)}), f32[32,64,128]{2,1,0:T(8,128)}, u32[]{:S(2)}, u32[]{:S(2)}) %all-to-all-start.2) | async-done | bytes 1048608 | tf_op jit(solution)/shard_map/all_to_all | solution.py:138
  246.7 6.1 %scatter_custom_fusion.3 = f32[1024,128]{1,0:T(8,128)S(1)} fusion(s32[2048]{0:T(1024)S(1)} %bitcast.14, f32[2048,128]{1,0:T(8,128)} %bitcast.7, f32[]{:T(128)} %constant.88.clone.1), kind=kCustom, calls=%fused_computation.118 | custom fusion | bytes 524800 | tf_op jit(solution)/shard_map/scatter | solution.py:146
  (129 shorter events, 61.5 us)
Async XLA Ops:
  10.3 74.6 %copy-start = (f32[1024,128]{1,0:T(8,128)S(1)}, f32[1024,128]{1,0:T(8,128)}, u32[]{:S(2)}) copy-start(f32[1024,128]{1,0:T(8,128)} %param.13) | copy-start | bytes 1572868
  61.1 4.3 %copy-start.6 = (s32[16,64]{1,0:T(8,128)S(1)}, s32[16,64]{1,0:T(8,128)}, u32[]{:S(2)}) copy-start(s32[16,64]{1,0:T(8,128)} %param.12) | copy-start | bytes 12292
  91.7 28.3 %all-to-all-start.1 = ((f32[32,64,128]{2,1,0:T(8,128)}), f32[32,64,128]{2,1,0:T(8,128)S(1)}, u32[]{:S(2)}, u32[]{:S(2)}) async-start(f32[32,64,128]{2,1,0:T(8,128)} %broadcast_select_fusion), calls=%async_computation.1 | async-start | bytes 2097152 | tf_op jit(solution)/shard_map/all_to_all | solution.py:125
  122.9 14.1 %copy-start.1 = (f32[16,64,128]{2,1,0:T(8,128)S(1)}, f32[16,64,128]{2,1,0:T(8,128)}, u32[]{:S(2)}) copy-start(f32[16,64,128]{2,1,0:T(8,128)} %param.9) | copy-start | bytes 1572868
  123.1 13.9 %collective-permute-start = (f32[1,64,128]{2,1,0:T(8,128)S(1)}, f32[1,64,128]{2,1,0:T(8,128)S(1)}, u32[]{:S(2)}, u32[]{:S(2)}) collective-permute-start(f32[1,64,128]{2,1,0:T(8,128)S(1)} %get-tuple-element.121), channel_id=1, source_target_pairs={{1,0},{2,1},{3,2},{5,4},{6,5},{7,6},{9,8},{10,9},{11,10},{13,12},{... | collective-permute-start | bytes 98312 | tf_op jit(solution)/shard_map/ppermute | solution.py:25
  126.2 10.8 %collective-permute-start.1 = (f32[1,64,128]{2,1,0:T(8,128)S(1)}, f32[1,64,128]{2,1,0:T(8,128)S(1)}, u32[]{:S(2)}, u32[]{:S(2)}) collective-permute-start(f32[1,64,128]{2,1,0:T(8,128)S(1)} %get-tuple-element.122), channel_id=1, source_target_pairs={{0,1},{1,2},{2,3},{4,5},{5,6},{6,7},{8,9},{9,10},{10,11},{12,13},{... | collective-permute-start | bytes 98312 | tf_op jit(solution)/shard_map/ppermute | solution.py:23
  129.2 3.1 %collective-permute-start.2 = (f32[16,1,128]{2,1,0:T(1,128)S(1)}, f32[16,1,128]{2,1,0:T(1,128)S(1)}, u32[]{:S(2)}, u32[]{:S(2)}) collective-permute-start(f32[16,1,128]{2,1,0:T(1,128)S(1)} %get-tuple-element.123), channel_id=1, source_target_pairs={{4,0},{8,4},{12,8},{16,12},{20,16},{24,20},{28,24},{0,28},{5,1},{9... | collective-permute-start | bytes 24584 | tf_op jit(solution)/shard_map/ppermute | solution.py:25
  131.5 5.5 %collective-permute-start.3 = (f32[16,1,128]{2,1,0:T(1,128)S(1)}, f32[16,1,128]{2,1,0:T(1,128)S(1)}, u32[]{:S(2)}, u32[]{:S(2)}) collective-permute-start(f32[16,1,128]{2,1,0:T(1,128)S(1)} %get-tuple-element.124), channel_id=1, source_target_pairs={{0,4},{4,8},{8,12},{12,16},{16,20},{20,24},{24,28},{28,0},{1,5},{5... | collective-permute-start | bytes 24584 | tf_op jit(solution)/shard_map/ppermute | solution.py:23
  137.5 10.9 %collective-permute-start.4 = (f32[1,64,128]{2,1,0:T(8,128)S(1)}, f32[1,64,128]{2,1,0:T(8,128)S(1)}, u32[]{:S(2)}, u32[]{:S(2)}) collective-permute-start(f32[1,64,128]{2,1,0:T(8,128)S(1)} %get-tuple-element.117), channel_id=1, source_target_pairs={{1,0},{2,1},{3,2},{5,4},{6,5},{7,6},{9,8},{10,9},{11,10},{13,12},{... | collective-permute-start | bytes 98312 | tf_op jit(solution)/shard_map/ppermute | solution.py:25
  139.8 8.6 %collective-permute-start.5 = (f32[1,64,128]{2,1,0:T(8,128)S(1)}, f32[1,64,128]{2,1,0:T(8,128)S(1)}, u32[]{:S(2)}, u32[]{:S(2)}) collective-permute-start(f32[1,64,128]{2,1,0:T(8,128)S(1)} %get-tuple-element.118), channel_id=1, source_target_pairs={{0,1},{1,2},{2,3},{4,5},{5,6},{6,7},{8,9},{9,10},{10,11},{12,13},{... | collective-permute-start | bytes 98312 | tf_op jit(solution)/shard_map/ppermute | solution.py:23
  143.1 2.6 %collective-permute-start.6 = (f32[16,1,128]{2,1,0:T(1,128)S(1)}, f32[16,1,128]{2,1,0:T(1,128)S(1)}, u32[]{:S(2)}, u32[]{:S(2)}) collective-permute-start(f32[16,1,128]{2,1,0:T(1,128)S(1)} %get-tuple-element.119), channel_id=1, source_target_pairs={{4,0},{8,4},{12,8},{16,12},{20,16},{24,20},{28,24},{0,28},{5,1},{9... | collective-permute-start | bytes 24584 | tf_op jit(solution)/shard_map/ppermute | solution.py:25
  143.2 5.3 %collective-permute-start.7 = (f32[16,1,128]{2,1,0:T(1,128)S(1)}, f32[16,1,128]{2,1,0:T(1,128)S(1)}, u32[]{:S(2)}, u32[]{:S(2)}) collective-permute-start(f32[16,1,128]{2,1,0:T(1,128)S(1)} %get-tuple-element.120), channel_id=1, source_target_pairs={{0,4},{4,8},{8,12},{12,16},{16,20},{20,24},{24,28},{28,0},{1,5},{5... | collective-permute-start | bytes 24584 | tf_op jit(solution)/shard_map/ppermute | solution.py:23
  149.3 10.9 %collective-permute-start.8 = (f32[1,64,128]{2,1,0:T(8,128)S(1)}, f32[1,64,128]{2,1,0:T(8,128)S(1)}, u32[]{:S(2)}, u32[]{:S(2)}) collective-permute-start(f32[1,64,128]{2,1,0:T(8,128)S(1)} %get-tuple-element.113), channel_id=1, source_target_pairs={{1,0},{2,1},{3,2},{5,4},{6,5},{7,6},{9,8},{10,9},{11,10},{13,12},{... | collective-permute-start | bytes 98312 | tf_op jit(solution)/shard_map/ppermute | solution.py:25
  151.5 8.7 %collective-permute-start.9 = (f32[1,64,128]{2,1,0:T(8,128)S(1)}, f32[1,64,128]{2,1,0:T(8,128)S(1)}, u32[]{:S(2)}, u32[]{:S(2)}) collective-permute-start(f32[1,64,128]{2,1,0:T(8,128)S(1)} %get-tuple-element.114), channel_id=1, source_target_pairs={{0,1},{1,2},{2,3},{4,5},{5,6},{6,7},{8,9},{9,10},{10,11},{12,13},{... | collective-permute-start | bytes 98312 | tf_op jit(solution)/shard_map/ppermute | solution.py:23
  154.9 2.6 %collective-permute-start.10 = (f32[16,1,128]{2,1,0:T(1,128)S(1)}, f32[16,1,128]{2,1,0:T(1,128)S(1)}, u32[]{:S(2)}, u32[]{:S(2)}) collective-permute-start(f32[16,1,128]{2,1,0:T(1,128)S(1)} %get-tuple-element.115), channel_id=1, source_target_pairs={{4,0},{8,4},{12,8},{16,12},{20,16},{24,20},{28,24},{0,28},{5,1},{9... | collective-permute-start | bytes 24584 | tf_op jit(solution)/shard_map/ppermute | solution.py:25
  154.9 5.3 %collective-permute-start.11 = (f32[16,1,128]{2,1,0:T(1,128)S(1)}, f32[16,1,128]{2,1,0:T(1,128)S(1)}, u32[]{:S(2)}, u32[]{:S(2)}) collective-permute-start(f32[16,1,128]{2,1,0:T(1,128)S(1)} %get-tuple-element.116), channel_id=1, source_target_pairs={{0,4},{4,8},{8,12},{12,16},{16,20},{20,24},{24,28},{28,0},{1,5},{5... | collective-permute-start | bytes 24584 | tf_op jit(solution)/shard_map/ppermute | solution.py:23
  161.1 12.1 %copy-start.2 = (f32[16,64,128]{2,1,0:T(8,128)}, f32[16,64,128]{2,1,0:T(8,128)S(1)}, u32[]{:S(2)}) copy-start(f32[16,64,128]{2,1,0:T(8,128)S(1)} %fusion.25) | copy-start | bytes 1572868
  161.1 10.9 %collective-permute-start.12 = (f32[1,64,128]{2,1,0:T(8,128)S(1)}, f32[1,64,128]{2,1,0:T(8,128)S(1)}, u32[]{:S(2)}, u32[]{:S(2)}) collective-permute-start(f32[1,64,128]{2,1,0:T(8,128)S(1)} %get-tuple-element.107), channel_id=1, source_target_pairs={{1,0},{2,1},{3,2},{5,4},{6,5},{7,6},{9,8},{10,9},{11,10},{13,12},{... | collective-permute-start | bytes 98312 | tf_op jit(solution)/shard_map/ppermute | solution.py:25
  163.3 8.8 %collective-permute-start.13 = (f32[1,64,128]{2,1,0:T(8,128)S(1)}, f32[1,64,128]{2,1,0:T(8,128)S(1)}, u32[]{:S(2)}, u32[]{:S(2)}) collective-permute-start(f32[1,64,128]{2,1,0:T(8,128)S(1)} %get-tuple-element.108), channel_id=1, source_target_pairs={{0,1},{1,2},{2,3},{4,5},{5,6},{6,7},{8,9},{9,10},{10,11},{12,13},{... | collective-permute-start | bytes 98312 | tf_op jit(solution)/shard_map/ppermute | solution.py:23
  166.7 2.6 %collective-permute-start.14 = (f32[16,1,128]{2,1,0:T(1,128)S(1)}, f32[16,1,128]{2,1,0:T(1,128)S(1)}, u32[]{:S(2)}, u32[]{:S(2)}) collective-permute-start(f32[16,1,128]{2,1,0:T(1,128)S(1)} %get-tuple-element.109), channel_id=1, source_target_pairs={{4,0},{8,4},{12,8},{16,12},{20,16},{24,20},{28,24},{0,28},{5,1},{9... | collective-permute-start | bytes 24584 | tf_op jit(solution)/shard_map/ppermute | solution.py:25
  166.8 5.3 %collective-permute-start.15 = (f32[16,1,128]{2,1,0:T(1,128)S(1)}, f32[16,1,128]{2,1,0:T(1,128)S(1)}, u32[]{:S(2)}, u32[]{:S(2)}) collective-permute-start(f32[16,1,128]{2,1,0:T(1,128)S(1)} %get-tuple-element.110), channel_id=1, source_target_pairs={{0,4},{4,8},{8,12},{12,16},{16,20},{20,24},{24,28},{28,0},{1,5},{5... | collective-permute-start | bytes 24584 | tf_op jit(solution)/shard_map/ppermute | solution.py:23
  214.0 7.3 %copy-start.4 = (f32[1024,128]{1,0:T(8,128)S(1)}, f32[1024,128]{1,0:T(8,128)}, u32[]{:S(2)}) copy-start(f32[1024,128]{1,0:T(8,128)} %param.15) | copy-start | bytes 1572868
  214.0 32.7 %all-to-all-start.2 = ((f32[32,64,128]{2,1,0:T(8,128)}), f32[32,64,128]{2,1,0:T(8,128)}, u32[]{:S(2)}, u32[]{:S(2)}) async-start(f32[32,64,128]{2,1,0:T(8,128)} %bitcast.6), calls=%async_computation.2 | async-start | bytes 2097152 | tf_op jit(solution)/shard_map/all_to_all | solution.py:138
  221.7 31.0 %copy-start.3 = (f32[1024,128]{1,0:T(8,128)S(1)}, f32[1024,128]{1,0:T(8,128)}, u32[]{:S(2)}) copy-start(f32[1024,128]{1,0:T(8,128)} %param.14) | copy-start | bytes 1572868
  (1 other events, 2.8 us)
where the time goes:
time: 256 us; the launch traced here: 255 us
  local copies, waits for them, and re-layouts  83.5 us (33%)
  waiting for transfers between devices  67.2 us (26%)
  blocking collectives  49.6 us (19%)
  starting transfers between devices  39.8 us (16%)
  other arithmetic  12.2 us (5%)
    gather x11, local copies, waits for them, and re-layouts, send_places(): run_start = jnp.searchsorted(ranked, ranked, side='left')  49.8 us
    psum x1, blocking collectives, per_device(): total = lax.psum(jnp.sum(power), ('blk', 'layer'))  36 us
    all_to_all x1, waiting for transfers between devices, per_device(): lax.all_to_all(replies, ('blk', 'layer'), split_axis=0, concat_axis=0, ti...  25.4 us
    all_to_all x1, waiting for transfers between devices, per_device(): lax.all_to_all(outgoing.reshape(peers, capacity, radial), ('blk', 'layer'...  24.9 us
    ppermute x8, starting transfers between devices, with_halo(): lax.ppermute(tail, axis, [(i, (i + 1) % count) for i in range(ends)])  17.4 us
    all_to_all x1, blocking collectives, per_device(): lax.all_to_all(outgoing_slots.reshape(peers, capacity), ('blk', 'layer'),...  13.7 us
    ppermute x8, waiting for transfers between devices, with_halo(): lax.ppermute(tail, axis, [(i, (i + 1) % count) for i in range(ends)])  13 us
    ppermute x8, starting transfers between devices, with_halo(): lax.ppermute(head, axis, [((i + 1) % count, i) for i in range(ends)])  12.2 us
  transfers between devices with their start and end apart: 18, of which 10 were waited for; matrix products, arithmetic and copies ran while one was open for 0% of the time, Pallas kernels for 0%

commit v1 on v0

--- a/solution.py
+++ b/solution.py
@@ -92,58 +92,73 @@
     return current
 
 
-def send_places(owner, peers):
+def routing(owner, slot, peers):
     owners = owner.reshape(-1)
-    block_count = owners.shape[0]
-    capacity = 2 * block_count // peers
-    ordering = jnp.argsort(owners, stable=True)
-    ranked = owners[ordering]
-    run_start = jnp.searchsorted(ranked, ranked, side="left")
-    placed = jnp.arange(block_count, dtype=jnp.int32) - run_start
-    within = jnp.zeros((block_count,), jnp.int32).at[ordering].set(placed)
-    return (owners * capacity + within, capacity)
+    slots = slot.reshape(-1)
+    count = owners.shape[0]
+    capacity = 2 * count // peers
+    named = owners[:, None] == jnp.arange(peers, dtype=jnp.int32)[None, :]
+    named_bf = named.astype(jnp.bfloat16)
+    order = jnp.arange(count, dtype=jnp.int32)
+    earlier = (order[None, :] < order[:, None]).astype(jnp.bfloat16)
+    before = jnp.dot(earlier, named_bf, preferred_element_type=jnp.float32)
+    within = jnp.sum(jnp.where(named, before, 0.0), axis=1).astype(jnp.int32)
+    here = within[:, None] == jnp.arange(capacity, dtype=jnp.int32)[None, :]
+    parts = []
+    for code in (slots + 1, order + 1):
+        for digit in (code >> 5, code & 31):
+            parts.append(jnp.where(here, digit[:, None].astype(jnp.float32), 0.0))
+    table = jnp.concatenate(parts, axis=1).astype(jnp.bfloat16)
+    digits = lax.dot_general(
+        named_bf, table, (((0,), (0,)), ((), ())), preferred_element_type=jnp.float32
+    ).astype(jnp.int32).reshape(peers, 4, capacity)
+    slot_code = digits[:, 0] * 32 + digits[:, 1]
+    block_code = digits[:, 2] * 32 + digits[:, 3]
+    return owners * capacity + within, slot_code, block_code
+
+
+def arrivals(slot_code, count):
+    code = slot_code.reshape(-1) - 1
+    total = code.shape[0]
+    place = jnp.arange(total, dtype=jnp.int32)
+    low = (code & 31)[:, None] == jnp.arange(32, dtype=jnp.int32)[None, :]
+    high = ((code >> 5)[:, None] == jnp.arange(count // 32, dtype=jnp.int32)[None, :])
+    table = jnp.concatenate(
+        [jnp.where(low, d[:, None].astype(jnp.float32), 0.0) for d in (place >> 5, place & 31)],
+        axis=1,
+    ).astype(jnp.bfloat16)
+    digits = lax.dot_general(
+        high.astype(jnp.bfloat16), table, (((0,), (0,)), ((), ())),
+        preferred_element_type=jnp.float32,
+    ).astype(jnp.int32)
+    return (digits[:, :32] * 32 + digits[:, 32:]).reshape(-1)
+
+
+def swap(rows):
+    return lax.all_to_all(rows, ("blk", "layer"), split_axis=0, concat_axis=0, tiled=True)
 
 
 def per_device(source, sigma_ref, owner, slot, temp_old, heat_cap, conduct):
     peers = lax.axis_size(("blk", "layer"))
     radial = source.shape[2]
     block_count = temp_old.shape[0]
-    positions, capacity = send_places(owner, peers)
-    outgoing_slots = (
-        jnp.full((peers * capacity,), block_count, jnp.int32).at[positions].set(slot.reshape(-1))
-    )
-    wanted = lax.all_to_all(
-        outgoing_slots.reshape(peers, capacity),
-        ("blk", "layer"),
-        split_axis=0,
-        concat_axis=0,
-        tiled=True,
-    ).reshape(-1)
-    replies = jnp.take(temp_old, wanted, axis=0, mode="fill", fill_value=0.0).reshape(
-        peers, capacity, radial
-    )
-    fetched = lax.all_to_all(replies, ("blk", "layer"), split_axis=0, concat_axis=0, tiled=True)
-    temp_here = jnp.take(fetched.reshape(-1, radial), positions, axis=0).reshape(source.shape)
+    positions, slot_code, block_code = routing(owner, slot, peers)
+    capacity = slot_code.shape[1]
+    wanted = swap(slot_code)
+    replies = jnp.take(temp_old, jnp.maximum(wanted.reshape(-1) - 1, 0), axis=0, mode="clip")
+    fetched = swap(replies.reshape(peers, capacity, radial)).reshape(-1, radial)
+    origin = arrivals(wanted, block_count)
+    temp_here = jnp.take(fetched, positions, axis=0, mode="clip").reshape(source.shape)
     cond_here = sigma_ref / (1.0 + COUPLE * temp_here)
     potential = electric(source, cond_here)
     power = joule(potential, cond_here)
     total = lax.psum(jnp.sum(power), ("blk", "layer"))
+    outgoing = jnp.take(
+        power.reshape(-1, radial), jnp.maximum(block_code.reshape(-1) - 1, 0), axis=0, mode="clip"
+    )
+    arrived = swap(outgoing.reshape(peers, capacity, radial)).reshape(-1, radial)
     factor = source.size * peers / total
-    power = power * factor
-    outgoing = (
-        jnp.zeros((peers * capacity, radial), jnp.float32)
-        .at[positions]
-        .set(power.reshape(-1, radial))
-    )
-    arrived = lax.all_to_all(
-        outgoing.reshape(peers, capacity, radial),
-        ("blk", "layer"),
-        split_axis=0,
-        concat_axis=0,
-        tiled=True,
-    )
-    arrived = arrived.reshape(-1, radial)
-    heat = jnp.zeros((block_count, radial), jnp.float32).at[wanted].set(arrived, mode="drop")
+    heat = jnp.take(arrived, origin, axis=0, mode="clip") * factor
     temp_new = thermal_step(temp_old, heat_cap, conduct, heat)
     return (potential, temp_new)
 

time: 256 us -> 173 us (0.68)
  local copies, waits for them, and re-layouts: 83.5 us -> 24.6 us
  waiting for transfers between devices: 67.2 us -> 42.2 us
  blocking collectives: 49.6 us -> 55 us
  starting transfers between devices: 39.8 us -> 35.1 us
    gather x14 -> x4, local copies, waits for them, and re-layouts: 62.6 us -> 20.7 us  [the longest x1 7.56 us: per_device(): jnp.take(temp_old, jnp.maximum(wanted.reshape(-1) - 1, 0), axis=0, mode='...]
    all_to_all x2, waiting for transfers between devices: 50.3 us -> 25.3 us  [swap(): lax.all_to_all(rows, ('blk', 'layer'), split_axis=0, concat_axis=0, tiled...]
    scatter x4 -> x0, local copies, waits for them, and re-layouts: 18.8 us -> none  [the longest x1 6.08 us: per_device(): jnp.zeros((block_count, radial), jnp.float32).at[wanted]]
    psum x1, blocking collectives: 36 us -> 41.3 us  [per_device(): total = lax.psum(jnp.sum(power), ('blk', 'layer'))]
    all_to_all x2, starting transfers between devices: 10.2 us -> 5.54 us  [swap(): lax.all_to_all(rows, ('blk', 'layer'), split_axis=0, concat_axis=0, tiled...]
    sort x1 -> x0, other arithmetic: 4.37 us -> none  [send_places(): ordering = jnp.argsort(owners, stable=True)]
    another operation x0 -> x2, other arithmetic: none -> 2.58 us
  transfers between devices with their start and end apart: 18 -> 18, of which waited for: 10 -> 9; matrix products, arithmetic and copies ran while one was open for 0% -> 2% of each run, Pallas kernels for 0% -> 0%
where the time goes in v1:
time: 173 us; the launch traced here: 172 us
  blocking collectives  55 us (32%)
  waiting for transfers between devices  42.2 us (24%)
  starting transfers between devices  35.1 us (20%)
  local copies, waits for them, and re-layouts  24.6 us (14%)
  other arithmetic  11.2 us (6%)
  matrix products  1.86 us (1%)
    psum x1, blocking collectives, per_device(): total = lax.psum(jnp.sum(power), ('blk', 'layer'))  41.3 us
    all_to_all x2, waiting for transfers between devices, swap(): lax.all_to_all(rows, ('blk', 'layer'), split_axis=0, concat_axis=0, tiled...  25.3 us
    ppermute x8, starting transfers between devices, with_halo(): lax.ppermute(tail, axis, [(i, (i + 1) % count) for i in range(ends)])  17.4 us
    all_to_all x1, blocking collectives, swap(): lax.all_to_all(rows, ('blk', 'layer'), split_axis=0, concat_axis=0, tiled...  13.7 us
    ppermute x8, waiting for transfers between devices, with_halo(): lax.ppermute(tail, axis, [(i, (i + 1) % count) for i in range(ends)])  13 us
    ppermute x8, starting transfers between devices, with_halo(): lax.ppermute(head, axis, [((i + 1) % count, i) for i in range(ends)])  12.1 us
    gather x1, local copies, waits for them, and re-layouts, per_device(): jnp.take(temp_old, jnp.maximum(wanted.reshape(-1) - 1, 0), axis=0, mode='...  7.56 us
    gather x1, local copies, waits for them, and re-layouts, per_device(): jnp.take(power.reshape(-1, radial), jnp.maximum(block_code.reshape(-1) -...  7.56 us
  transfers between devices with their start and end apart: 18, of which 9 were waited for; matrix products, arithmetic and copies ran while one was open for 2% of the time, Pallas kernels for 0%

profile of v1, /device:TPU:1, one launch (start us, length us, event | category | flops | bytes accessed | tf_op | source)
XLA Modules:
  0.0 171.5 jit_solution(1964894668424559672)
XLA Ops:
  3.8 13.7 %all_to_all.16 = s32[32,1,64]{2,1,0:T(1,128)S(1)} all-to-all(s32[32,1,64]{2,1,0:T(1,128)S(1)} %get-tuple-element.32), channel_id=1, replica_groups=mesh['blk'=8,'layer'=4] {'blk','layer'}, dimensions={0} | all-to-all | bytes 16384 | tf_op jit(solution)/shard_map/all_to_all | solution.py:138
  17.8 7.6 %gather_fusion = f32[2048,128]{1,0:T(8,128)} fusion(f32[1024,128]{1,0:T(8,128)S(1)} %copy-done, s32[2048]{0:T(1024)S(1)} %broadcast_clamp_fusion.1), kind=kCustom, calls=%fused_computation | custom fusion | bytes 2105344 | tf_op jit(solution)/shard_map/jit(_take)/gather | solution.py:148
  25.3 3.0 %all-to-all-start.1 = ((f32[32,64,128]{2,1,0:T(8,128)}), f32[32,64,128]{2,1,0:T(8,128)S(1)}, u32[]{:S(2)}, u32[]{:S(2)}) async-start(f32[32,64,128]{2,1,0:T(8,128)} %bitcast), calls=%async_computation.1 | async-start | bytes 2097152 | tf_op jit(solution)/shard_map/all_to_all | solution.py:138
  28.5 25.3 %all-to-all-done.1 = f32[32,64,128]{2,1,0:T(8,128)S(1)} async-done(((f32[32,64,128]{2,1,0:T(8,128)}), f32[32,64,128]{2,1,0:T(8,128)S(1)}, u32[]{:S(2)}, u32[]{:S(2)}) %all-to-all-start.1) | async-done | bytes 1048608 | tf_op jit(solution)/shard_map/all_to_all | solution.py:138
  53.8 2.8 %gather_fusion.1 = f32[1024,128]{1,0:T(8,128)S(1)} fusion(f32[2048,128]{1,0:T(8,128)S(1)} %bitcast.10, s32[1024]{0:T(1024)S(1)} %broadcast_clamp_fusion.3), kind=kCustom, calls=%fused_computation.1 | custom fusion | bytes 1052672 | tf_op jit(solution)/shard_map/jit(_take)/gather | solution.py:151
  57.7 3.1 %collective-permute-start = (f32[1,64,128]{2,1,0:T(8,128)S(1)}, f32[1,64,128]{2,1,0:T(8,128)S(1)}, u32[]{:S(2)}, u32[]{:S(2)}) collective-permute-start(f32[1,64,128]{2,1,0:T(8,128)S(1)} %get-tuple-element.27), channel_id=1, source_target_pairs={{1,0},{2,1},{3,2},{5,4},{6,5},{7,6},{9,8},{10,9},{11,10},{13,12},{... | collective-permute-start | bytes 98312 | tf_op jit(solution)/shard_map/ppermute | solution.py:25
  60.8 3.0 %collective-permute-start.1 = (f32[1,64,128]{2,1,0:T(8,128)S(1)}, f32[1,64,128]{2,1,0:T(8,128)S(1)}, u32[]{:S(2)}, u32[]{:S(2)}) collective-permute-start(f32[1,64,128]{2,1,0:T(8,128)S(1)} %get-tuple-element.28), channel_id=1, source_target_pairs={{0,1},{1,2},{2,3},{4,5},{5,6},{6,7},{8,9},{9,10},{10,11},{12,13},{... | collective-permute-start | bytes 98312 | tf_op jit(solution)/shard_map/ppermute | solution.py:23
  63.9 2.3 %collective-permute-start.2 = (f32[16,1,128]{2,1,0:T(1,128)S(1)}, f32[16,1,128]{2,1,0:T(1,128)S(1)}, u32[]{:S(2)}, u32[]{:S(2)}) collective-permute-start(f32[16,1,128]{2,1,0:T(1,128)S(1)} %get-tuple-element.29), channel_id=1, source_target_pairs={{4,0},{8,4},{12,8},{16,12},{20,16},{24,20},{28,24},{0,28},{5,1},{9... | collective-permute-start | bytes 24584 | tf_op jit(solution)/shard_map/ppermute | solution.py:25
  66.9 4.7 %collective-permute-done.3 = f32[16,1,128]{2,1,0:T(1,128)S(1)} collective-permute-done((f32[16,1,128]{2,1,0:T(1,128)S(1)}, f32[16,1,128]{2,1,0:T(1,128)S(1)}, u32[]{:S(2)}, u32[]{:S(2)}) %collective-permute-start.3) | collective-permute-done | bytes 8224 | tf_op jit(solution)/shard_map/ppermute | solution.py:23
  72.1 2.3 %collective-permute-start.4 = (f32[1,64,128]{2,1,0:T(8,128)S(1)}, f32[1,64,128]{2,1,0:T(8,128)S(1)}, u32[]{:S(2)}, u32[]{:S(2)}) collective-permute-start(f32[1,64,128]{2,1,0:T(8,128)S(1)} %get-tuple-element.23), channel_id=1, source_target_pairs={{1,0},{2,1},{3,2},{5,4},{6,5},{7,6},{9,8},{10,9},{11,10},{13,12},{... | collective-permute-start | bytes 98312 | tf_op jit(solution)/shard_map/ppermute | solution.py:25
  74.4 3.3 %collective-permute-start.5 = (f32[1,64,128]{2,1,0:T(8,128)S(1)}, f32[1,64,128]{2,1,0:T(8,128)S(1)}, u32[]{:S(2)}, u32[]{:S(2)}) collective-permute-start(f32[1,64,128]{2,1,0:T(8,128)S(1)} %get-tuple-element.24), channel_id=1, source_target_pairs={{0,1},{1,2},{2,3},{4,5},{5,6},{6,7},{8,9},{9,10},{10,11},{12,13},{... | collective-permute-start | bytes 98312 | tf_op jit(solution)/shard_map/ppermute | solution.py:23
  80.3 2.8 %collective-permute-done.7 = f32[16,1,128]{2,1,0:T(1,128)S(1)} collective-permute-done((f32[16,1,128]{2,1,0:T(1,128)S(1)}, f32[16,1,128]{2,1,0:T(1,128)S(1)}, u32[]{:S(2)}, u32[]{:S(2)}) %collective-permute-start.7) | collective-permute-done | bytes 8224 | tf_op jit(solution)/shard_map/ppermute | solution.py:23
  83.0 1.6 multiply_add_fusion.1
  84.7 2.2 %collective-permute-start.8 = (f32[1,64,128]{2,1,0:T(8,128)S(1)}, f32[1,64,128]{2,1,0:T(8,128)S(1)}, u32[]{:S(2)}, u32[]{:S(2)}) collective-permute-start(f32[1,64,128]{2,1,0:T(8,128)S(1)} %get-tuple-element.19), channel_id=1, source_target_pairs={{1,0},{2,1},{3,2},{5,4},{6,5},{7,6},{9,8},{10,9},{11,10},{13,12},{... | collective-permute-start | bytes 98312 | tf_op jit(solution)/shard_map/ppermute | solution.py:25
  86.9 3.3 %collective-permute-start.9 = (f32[1,64,128]{2,1,0:T(8,128)S(1)}, f32[1,64,128]{2,1,0:T(8,128)S(1)}, u32[]{:S(2)}, u32[]{:S(2)}) collective-permute-start(f32[1,64,128]{2,1,0:T(8,128)S(1)} %get-tuple-element.20), channel_id=1, source_target_pairs={{0,1},{1,2},{2,3},{4,5},{5,6},{6,7},{8,9},{9,10},{10,11},{12,13},{... | collective-permute-start | bytes 98312 | tf_op jit(solution)/shard_map/ppermute | solution.py:23
  92.8 2.8 %collective-permute-done.11 = f32[16,1,128]{2,1,0:T(1,128)S(1)} collective-permute-done((f32[16,1,128]{2,1,0:T(1,128)S(1)}, f32[16,1,128]{2,1,0:T(1,128)S(1)}, u32[]{:S(2)}, u32[]{:S(2)}) %collective-permute-start.11) | collective-permute-done | bytes 8224 | tf_op jit(solution)/shard_map/ppermute | solution.py:23
  95.6 1.9 %fusion.28 = f32[16,64,128]{2,1,0:T(8,128)S(1)} fusion(f32[16,64,128]{2,1,0:T(8,128)S(1)} %get-tuple-element.10, f32[16,64,128]{2,1,0:T(8,128)} %get-tuple-element.8, f32[16,64,128]{2,1,0:T(8,128)S(1)} %get-tuple-element.7, f32[16,1,128]{2,1,0:T(1,128)S(1)} %collective-permute-done.11, f32[16,1,128]{2,1,0:T(1,128)S(1)} %collective-permute-done.10, ...), kind=kLoop, calls=%fused_computation.53 | loop fusion | flops 6029312 | bytes 3309568 | tf_op jit(solution)/shard_map/add | solution.py:58
  97.5 2.1 %collective-permute-start.12 = (f32[1,64,128]{2,1,0:T(8,128)S(1)}, f32[1,64,128]{2,1,0:T(8,128)S(1)}, u32[]{:S(2)}, u32[]{:S(2)}) collective-permute-start(f32[1,64,128]{2,1,0:T(8,128)S(1)} %get-tuple-element.13), channel_id=1, source_target_pairs={{1,0},{2,1},{3,2},{5,4},{6,5},{7,6},{9,8},{10,9},{11,10},{13,12},{... | collective-permute-start | bytes 98312 | tf_op jit(solution)/shard_map/ppermute | solution.py:25
  99.7 3.4 %collective-permute-start.13 = (f32[1,64,128]{2,1,0:T(8,128)S(1)}, f32[1,64,128]{2,1,0:T(8,128)S(1)}, u32[]{:S(2)}, u32[]{:S(2)}) collective-permute-start(f32[1,64,128]{2,1,0:T(8,128)S(1)} %get-tuple-element.14), channel_id=1, source_target_pairs={{0,1},{1,2},{2,3},{4,5},{5,6},{6,7},{8,9},{9,10},{10,11},{12,13},{... | collective-permute-start | bytes 98312 | tf_op jit(solution)/shard_map/ppermute | solution.py:23
  105.7 2.8 %collective-permute-done.15 = f32[16,1,128]{2,1,0:T(1,128)S(1)} collective-permute-done((f32[16,1,128]{2,1,0:T(1,128)S(1)}, f32[16,1,128]{2,1,0:T(1,128)S(1)}, u32[]{:S(2)}, u32[]{:S(2)}) %collective-permute-start.15) | collective-permute-done | bytes 8224 | tf_op jit(solution)/shard_map/ppermute | solution.py:23
  109.6 7.6 %gather_fusion.2 = f32[2048,128]{1,0:T(8,128)} fusion(f32[1024,128]{1,0:T(8,128)S(1)} %bitcast.8, s32[2048]{0:T(1024)S(1)} %broadcast_clamp_fusion), kind=kCustom, calls=%fused_computation.2 | custom fusion | bytes 2105344 | tf_op jit(solution)/shard_map/jit(_take)/gather | solution.py:156
  117.2 2.5 %all-to-all-start.2 = ((f32[32,64,128]{2,1,0:T(8,128)}), f32[32,64,128]{2,1,0:T(8,128)S(1)}, u32[]{:S(2)}, u32[]{:S(2)}) async-start(f32[32,64,128]{2,1,0:T(8,128)} %bitcast.6), calls=%async_computation.2 | async-start | bytes 2097152 | tf_op jit(solution)/shard_map/all_to_all | solution.py:138
  123.8 41.3 %psum.7 = f32[]{:T(128)} all-reduce(f32[]{:T(128)} %get-tuple-element.5), channel_id=1, replica_groups=mesh['blk'=8,'layer'=4] {'blk','layer'}, use_global_device_ids=true, to_apply=%region_2.3 | all-reduce | flops 1 | bytes 8 | tf_op jit(solution)/shard_map/psum | solution.py:155
  165.8 2.8 %gather_fusion.3 = f32[1024,128]{1,0:T(8,128)S(1)} fusion(f32[2048,128]{1,0:T(8,128)S(1)} %bitcast.9, s32[1024]{0:T(1024)S(1)} %broadcast_clamp_fusion.2), kind=kCustom, calls=%fused_computation.3 | custom fusion | bytes 1052672 | tf_op jit(solution)/shard_map/jit(_take)/gather | solution.py:161
  (81 shorter events, 21.8 us)
Async XLA Ops:
  3.2 14.6 %copy-start = (f32[1024,128]{1,0:T(8,128)S(1)}, f32[1024,128]{1,0:T(8,128)}, u32[]{:S(2)}) copy-start(f32[1024,128]{1,0:T(8,128)} %param.11) | copy-start | bytes 1572868
  25.3 3.0 %copy-start.6 = (s32[16,64]{1,0:T(8,128)S(1)}, s32[16,64]{1,0:T(8,128)}, u32[]{:S(2)}) copy-start(s32[16,64]{1,0:T(8,128)} %param.9) | copy-start | bytes 12292
  25.3 28.5 %all-to-all-start.1 = ((f32[32,64,128]{2,1,0:T(8,128)}), f32[32,64,128]{2,1,0:T(8,128)S(1)}, u32[]{:S(2)}, u32[]{:S(2)}) async-start(f32[32,64,128]{2,1,0:T(8,128)} %bitcast), calls=%async_computation.1 | async-start | bytes 2097152 | tf_op jit(solution)/shard_map/all_to_all | solution.py:138
  56.7 15.0 %copy-start.1 = (f32[16,64,128]{2,1,0:T(8,128)S(1)}, f32[16,64,128]{2,1,0:T(8,128)}, u32[]{:S(2)}) copy-start(f32[16,64,128]{2,1,0:T(8,128)} %param.7) | copy-start | bytes 1572868
  57.7 13.9 %collective-permute-start = (f32[1,64,128]{2,1,0:T(8,128)S(1)}, f32[1,64,128]{2,1,0:T(8,128)S(1)}, u32[]{:S(2)}, u32[]{:S(2)}) collective-permute-start(f32[1,64,128]{2,1,0:T(8,128)S(1)} %get-tuple-element.27), channel_id=1, source_target_pairs={{1,0},{2,1},{3,2},{5,4},{6,5},{7,6},{9,8},{10,9},{11,10},{13,12},{... | collective-permute-start | bytes 98312 | tf_op jit(solution)/shard_map/ppermute | solution.py:25
  60.8 10.8 %collective-permute-start.1 = (f32[1,64,128]{2,1,0:T(8,128)S(1)}, f32[1,64,128]{2,1,0:T(8,128)S(1)}, u32[]{:S(2)}, u32[]{:S(2)}) collective-permute-start(f32[1,64,128]{2,1,0:T(8,128)S(1)} %get-tuple-element.28), channel_id=1, source_target_pairs={{0,1},{1,2},{2,3},{4,5},{5,6},{6,7},{8,9},{9,10},{10,11},{12,13},{... | collective-permute-start | bytes 98312 | tf_op jit(solution)/shard_map/ppermute | solution.py:23
  63.9 3.1 %collective-permute-start.2 = (f32[16,1,128]{2,1,0:T(1,128)S(1)}, f32[16,1,128]{2,1,0:T(1,128)S(1)}, u32[]{:S(2)}, u32[]{:S(2)}) collective-permute-start(f32[16,1,128]{2,1,0:T(1,128)S(1)} %get-tuple-element.29), channel_id=1, source_target_pairs={{4,0},{8,4},{12,8},{16,12},{20,16},{24,20},{28,24},{0,28},{5,1},{9... | collective-permute-start | bytes 24584 | tf_op jit(solution)/shard_map/ppermute | solution.py:25
  66.1 5.5 %collective-permute-start.3 = (f32[16,1,128]{2,1,0:T(1,128)S(1)}, f32[16,1,128]{2,1,0:T(1,128)S(1)}, u32[]{:S(2)}, u32[]{:S(2)}) collective-permute-start(f32[16,1,128]{2,1,0:T(1,128)S(1)} %get-tuple-element.30), channel_id=1, source_target_pairs={{0,4},{4,8},{8,12},{12,16},{16,20},{20,24},{24,28},{28,0},{1,5},{5... | collective-permute-start | bytes 24584 | tf_op jit(solution)/shard_map/ppermute | solution.py:23
  72.1 10.9 %collective-permute-start.4 = (f32[1,64,128]{2,1,0:T(8,128)S(1)}, f32[1,64,128]{2,1,0:T(8,128)S(1)}, u32[]{:S(2)}, u32[]{:S(2)}) collective-permute-start(f32[1,64,128]{2,1,0:T(8,128)S(1)} %get-tuple-element.23), channel_id=1, source_target_pairs={{1,0},{2,1},{3,2},{5,4},{6,5},{7,6},{9,8},{10,9},{11,10},{13,12},{... | collective-permute-start | bytes 98312 | tf_op jit(solution)/shard_map/ppermute | solution.py:25
  74.4 8.6 %collective-permute-start.5 = (f32[1,64,128]{2,1,0:T(8,128)S(1)}, f32[1,64,128]{2,1,0:T(8,128)S(1)}, u32[]{:S(2)}, u32[]{:S(2)}) collective-permute-start(f32[1,64,128]{2,1,0:T(8,128)S(1)} %get-tuple-element.24), channel_id=1, source_target_pairs={{0,1},{1,2},{2,3},{4,5},{5,6},{6,7},{8,9},{9,10},{10,11},{12,13},{... | collective-permute-start | bytes 98312 | tf_op jit(solution)/shard_map/ppermute | solution.py:23
  77.7 2.6 %collective-permute-start.6 = (f32[16,1,128]{2,1,0:T(1,128)S(1)}, f32[16,1,128]{2,1,0:T(1,128)S(1)}, u32[]{:S(2)}, u32[]{:S(2)}) collective-permute-start(f32[16,1,128]{2,1,0:T(1,128)S(1)} %get-tuple-element.25), channel_id=1, source_target_pairs={{4,0},{8,4},{12,8},{16,12},{20,16},{24,20},{28,24},{0,28},{5,1},{9... | collective-permute-start | bytes 24584 | tf_op jit(solution)/shard_map/ppermute | solution.py:25
  77.8 5.3 %collective-permute-start.7 = (f32[16,1,128]{2,1,0:T(1,128)S(1)}, f32[16,1,128]{2,1,0:T(1,128)S(1)}, u32[]{:S(2)}, u32[]{:S(2)}) collective-permute-start(f32[16,1,128]{2,1,0:T(1,128)S(1)} %get-tuple-element.26), channel_id=1, source_target_pairs={{0,4},{4,8},{8,12},{12,16},{16,20},{20,24},{24,28},{28,0},{1,5},{5... | collective-permute-start | bytes 24584 | tf_op jit(solution)/shard_map/ppermute | solution.py:23
  84.7 10.9 %collective-permute-start.8 = (f32[1,64,128]{2,1,0:T(8,128)S(1)}, f32[1,64,128]{2,1,0:T(8,128)S(1)}, u32[]{:S(2)}, u32[]{:S(2)}) collective-permute-start(f32[1,64,128]{2,1,0:T(8,128)S(1)} %get-tuple-element.19), channel_id=1, source_target_pairs={{1,0},{2,1},{3,2},{5,4},{6,5},{7,6},{9,8},{10,9},{11,10},{13,12},{... | collective-permute-start | bytes 98312 | tf_op jit(solution)/shard_map/ppermute | solution.py:25
  86.9 8.7 %collective-permute-start.9 = (f32[1,64,128]{2,1,0:T(8,128)S(1)}, f32[1,64,128]{2,1,0:T(8,128)S(1)}, u32[]{:S(2)}, u32[]{:S(2)}) collective-permute-start(f32[1,64,128]{2,1,0:T(8,128)S(1)} %get-tuple-element.20), channel_id=1, source_target_pairs={{0,1},{1,2},{2,3},{4,5},{5,6},{6,7},{8,9},{9,10},{10,11},{12,13},{... | collective-permute-start | bytes 98312 | tf_op jit(solution)/shard_map/ppermute | solution.py:23
  90.2 2.6 %collective-permute-start.10 = (f32[16,1,128]{2,1,0:T(1,128)S(1)}, f32[16,1,128]{2,1,0:T(1,128)S(1)}, u32[]{:S(2)}, u32[]{:S(2)}) collective-permute-start(f32[16,1,128]{2,1,0:T(1,128)S(1)} %get-tuple-element.21), channel_id=1, source_target_pairs={{4,0},{8,4},{12,8},{16,12},{20,16},{24,20},{28,24},{0,28},{5,1},{9... | collective-permute-start | bytes 24584 | tf_op jit(solution)/shard_map/ppermute | solution.py:25
  90.3 5.3 %collective-permute-start.11 = (f32[16,1,128]{2,1,0:T(1,128)S(1)}, f32[16,1,128]{2,1,0:T(1,128)S(1)}, u32[]{:S(2)}, u32[]{:S(2)}) collective-permute-start(f32[16,1,128]{2,1,0:T(1,128)S(1)} %get-tuple-element.22), channel_id=1, source_target_pairs={{0,4},{4,8},{8,12},{12,16},{16,20},{20,24},{24,28},{28,0},{1,5},{5... | collective-permute-start | bytes 24584 | tf_op jit(solution)/shard_map/ppermute | solution.py:23
  97.5 19.7 %copy-start.2 = (f32[16,64,128]{2,1,0:T(8,128)}, f32[16,64,128]{2,1,0:T(8,128)S(1)}, u32[]{:S(2)}) copy-start(f32[16,64,128]{2,1,0:T(8,128)S(1)} %fusion.28) | copy-start | bytes 1572868
  97.5 10.9 %collective-permute-start.12 = (f32[1,64,128]{2,1,0:T(8,128)S(1)}, f32[1,64,128]{2,1,0:T(8,128)S(1)}, u32[]{:S(2)}, u32[]{:S(2)}) collective-permute-start(f32[1,64,128]{2,1,0:T(8,128)S(1)} %get-tuple-element.13), channel_id=1, source_target_pairs={{1,0},{2,1},{3,2},{5,4},{6,5},{7,6},{9,8},{10,9},{11,10},{13,12},{... | collective-permute-start | bytes 98312 | tf_op jit(solution)/shard_map/ppermute | solution.py:25
  99.7 8.8 %collective-permute-start.13 = (f32[1,64,128]{2,1,0:T(8,128)S(1)}, f32[1,64,128]{2,1,0:T(8,128)S(1)}, u32[]{:S(2)}, u32[]{:S(2)}) collective-permute-start(f32[1,64,128]{2,1,0:T(8,128)S(1)} %get-tuple-element.14), channel_id=1, source_target_pairs={{0,1},{1,2},{2,3},{4,5},{5,6},{6,7},{8,9},{9,10},{10,11},{12,13},{... | collective-permute-start | bytes 98312 | tf_op jit(solution)/shard_map/ppermute | solution.py:23
  103.1 2.6 %collective-permute-start.14 = (f32[16,1,128]{2,1,0:T(1,128)S(1)}, f32[16,1,128]{2,1,0:T(1,128)S(1)}, u32[]{:S(2)}, u32[]{:S(2)}) collective-permute-start(f32[16,1,128]{2,1,0:T(1,128)S(1)} %get-tuple-element.15), channel_id=1, source_target_pairs={{4,0},{8,4},{12,8},{16,12},{20,16},{24,20},{28,24},{0,28},{5,1},{9... | collective-permute-start | bytes 24584 | tf_op jit(solution)/shard_map/ppermute | solution.py:25
  103.2 5.3 %collective-permute-start.15 = (f32[16,1,128]{2,1,0:T(1,128)S(1)}, f32[16,1,128]{2,1,0:T(1,128)S(1)}, u32[]{:S(2)}, u32[]{:S(2)}) collective-permute-start(f32[16,1,128]{2,1,0:T(1,128)S(1)} %get-tuple-element.16), channel_id=1, source_target_pairs={{0,4},{4,8},{8,12},{12,16},{16,20},{20,24},{24,28},{28,0},{1,5},{5... | collective-permute-start | bytes 24584 | tf_op jit(solution)/shard_map/ppermute | solution.py:23
  117.2 2.5 %copy-start.3 = (f32[1024,128]{1,0:T(8,128)S(1)}, f32[1024,128]{1,0:T(8,128)}, u32[]{:S(2)}) copy-start(f32[1024,128]{1,0:T(8,128)} %param.13) | copy-start | bytes 1572868
  117.2 48.5 %all-to-all-start.2 = ((f32[32,64,128]{2,1,0:T(8,128)}), f32[32,64,128]{2,1,0:T(8,128)S(1)}, u32[]{:S(2)}, u32[]{:S(2)}) async-start(f32[32,64,128]{2,1,0:T(8,128)} %bitcast.6), calls=%async_computation.2 | async-start | bytes 2097152 | tf_op jit(solution)/shard_map/all_to_all | solution.py:138
  165.7 2.8 %copy-start.4 = (f32[1024,128]{1,0:T(8,128)S(1)}, f32[1024,128]{1,0:T(8,128)}, u32[]{:S(2)}) copy-start(f32[1024,128]{1,0:T(8,128)} %param.12) | copy-start | bytes 1572868
  (2 other events, 2.4 us)

commit v2 on v1

v2 whole, which is shorter than its diff:
```python
import jax
import jax.numpy as jnp
from jax import lax
from jax.experimental import pallas as pl
from jax.experimental.pallas import tpu as pltpu
from jax.sharding import PartitionSpec as P

SWEEPS = 3
JACOBI = 2


COUPLE = 0.4
THETA = 1.125
DELTA = 0.875


def routing(owner, slot, peers):
    owners = owner.reshape(-1)
    slots = slot.reshape(-1)
    count = owners.shape[0]
    capacity = 2 * count // peers
    named = owners[:, None] == jnp.arange(peers, dtype=jnp.int32)[None, :]
    named_bf = named.astype(jnp.bfloat16)
    order = jnp.arange(count, dtype=jnp.int32)
    earlier = (order[None, :] < order[:, None]).astype(jnp.bfloat16)
    before = jnp.dot(earlier, named_bf, preferred_element_type=jnp.float32)
    within = jnp.sum(jnp.where(named, before, 0.0), axis=1).astype(jnp.int32)
    here = within[:, None] == jnp.arange(capacity, dtype=jnp.int32)[None, :]
    parts = []
    for code in (slots + 1, order + 1):
        for digit in (code >> 5, code & 31):
            parts.append(jnp.where(here, digit[:, None].astype(jnp.float32), 0.0))
    table = jnp.concatenate(parts, axis=1).astype(jnp.bfloat16)
    digits = lax.dot_general(
        named_bf, table, (((0,), (0,)), ((), ())), preferred_element_type=jnp.float32
    ).astype(jnp.int32).reshape(peers, 4, capacity)
    slot_code = digits[:, 0] * 32 + digits[:, 1]
    block_code = digits[:, 2] * 32 + digits[:, 3]
    return owners * capacity + within, slot_code, block_code


WIDE = 4
ROWS = 8
MESH = pl.DeviceIdType.MESH


def shifted(x, step, axis, bounded):
    size = x.shape[axis]
    moved = pltpu.roll(x, step % size, axis)
    if bounded:
        place = lax.broadcasted_iota(jnp.int32, x.shape, axis)
        moved = jnp.where(place == (0 if step > 0 else size - 1), 0.0, moved)
    return moved


def around(ref, e):
    here = ref[e]
    return here, [
        ref[e + 1],
        ref[e - 1],
        shifted(here, -1, 0, False),
        shifted(here, 1, 0, False),
        shifted(here, -1, 1, True),
        shifted(here, 1, 1, True),
    ]


def exchange_kernel(
    layers, blks, slabs,
    source, sigma, temp_old, ask, places, blocks,
    potential, arrived, wanted, sums,
    asked, rows, fetched, src, cond, inv, dir_a, dir_b, res, pot, power, part,
    local_sem, ask_send, ask_recv, row_send, row_recv, pow_send, pow_recv, sum_send, sum_recv,
    halo_send, halo_recv,
):
    n = layers * blks
    cap = blocks.shape[1]
    ca, cr, lanes = source.shape
    blk, layer = lax.axis_index("blk"), lax.axis_index("layer")
    me = blk * layers + layer

    def peer(j):
        return (j // layers, j % layers)

    barrier = pltpu.get_barrier_semaphore()

    def greet(k, carry):
        pl.semaphore_signal(
            barrier, inc=1, device_id=peer(lax.rem(me + k, n)), device_id_type=MESH
        )
        return carry

    lax.fori_loop(1, n, greet, 0)
    own_src = pltpu.make_async_copy(
        source, src.at[pl.ds(WIDE, ca), pl.ds(ROWS, cr)], local_sem.at[0]
    )
    own_src.start()
    own_ask = pltpu.make_async_copy(ask.at[me], wanted.at[me], local_sem.at[1])
    own_ask.start()
    pl.semaphore_wait(barrier, n - 1)

    def remote(src_ref, dst_ref, send, recv, j):
        return pltpu.make_async_remote_copy(
            src_ref=src_ref, dst_ref=dst_ref, send_sem=send, recv_sem=recv,
            device_id=peer(j), device_id_type=MESH,
        )

    def ask_copy(j, slot):
        return remote(ask.at[j], wanted.at[slot], ask_send.at[j], ask_recv.at[slot], j)

    def send_ask(k, carry):
        ask_copy(lax.rem(me + k, n), me).start()
        return carry

    lax.fori_loop(1, n, send_ask, 0)

    directions = [(a, r) for a in (-1, 0, 1) for r in (-1, 0, 1) if (a, r) != (0, 0)]

    def halo(kind, d, field, whole):
        step_a, step_r = directions[d]
        count_a = ca if step_a == 0 else WIDE
        count_r = cr if step_r == 0 else ROWS
        from_a = ca - WIDE if step_a > 0 else 0
        from_r = cr - ROWS if step_r > 0 else 0
        to_a = {0: WIDE, 1: 0, -1: WIDE + ca}[step_a]
        to_r = {0: ROWS, 1: 0, -1: ROWS + cr}[step_r]
        off_a, off_r = (0, 0) if whole is not None else (WIDE, ROWS)
        origin = field if whole is None else whole
        return pltpu.make_async_remote_copy(
            src_ref=origin.at[pl.ds(off_a + from_a, count_a), pl.ds(off_r + from_r, count_r)],
            dst_ref=field.at[pl.ds(to_a, count_a), pl.ds(to_r, count_r)],
            send_sem=halo_send.at[kind, d],
            recv_sem=halo_recv.at[kind, d],
            device_id=(lax.rem(blk + step_r + blks, blks), lax.rem(layer + step_a + layers, layers)),
            device_id_type=MESH,
        )

    def halo_all(kind, field, whole, begin):
        for d, (step_a, _) in enumerate(directions):
            def act(d=d, incoming=False):
                copy = halo(kind, d, field, whole)
                if begin:
                    copy.start()
                elif incoming:
                    copy.wait_recv()
                else:
                    copy.wait_send()

            goes = {0: None, 1: layer < layers - 1, -1: layer > 0}[step_a]
            comes = {0: None, 1: layer > 0, -1: layer < layers - 1}[step_a]
            for cond_here, incoming in ((goes, False), (comes, True)):
                if begin and incoming:
                    continue
                if cond_here is None:
                    act(d, incoming)
                else:
                    pl.when(cond_here)(lambda d=d, incoming=incoming: act(d, incoming))

    halo_all(0, src, source, True)
    own_ask.wait()

    def row_copy(j, slot):
        return remote(
            rows.at[pl.ds(pl.multiple_of(j * cap, 8), cap)],
            fetched.at[pl.ds(pl.multiple_of(slot * cap, 8), cap)],
            row_send.at[j], row_recv.at[slot], j,
        )

    def fill(target, base, table, get):
        for c in range(cap):
            target[pl.ds(base + c, 1), :] = get(jnp.maximum(table(c) - 1, 0))

    def reply(k, carry):
        j = lax.rem(me - k + n, n)

        @pl.when(k > 0)
        def _():
            ask_copy(j, j).wait_recv()

        to_scalar = pltpu.make_async_copy(wanted.at[j], asked.at[j], local_sem.at[2])
        to_scalar.start()
        to_scalar.wait()
        base = pl.multiple_of(j * cap, 8)

        @pl.when(k > 0)
        def _():
            fill(rows, base, lambda c: asked[j, 0, c], lambda i: temp_old[pl.ds(i, 1), :])
            row_copy(j, me).start()

        @pl.when(k == 0)
        def _():
            fill(fetched, base, lambda c: asked[j, 0, c], lambda i: temp_old[pl.ds(i, 1), :])

        return carry

    lax.fori_loop(0, n, reply, 0)

    def got_row(k, carry):
        j = lax.rem(me + k, n)
        row_copy(j, j).wait_recv()
        return carry

    lax.fori_loop(1, n, got_row, 0)

    def place(a, carry):
        for r in range(cr):
            cond[WIDE + a, pl.ds(ROWS + r, 1), :] = fetched[pl.ds(places[a, r], 1), :]
        here = cond[WIDE + a, pl.ds(ROWS, cr), :]
        cond[WIDE + a, pl.ds(ROWS, cr), :] = sigma[a] / (1.0 + COUPLE * here)
        return carry

    lax.fori_loop(0, ca, place, 0)
    halo_all(1, cond, None, True)

    @pl.when(layer == 0)
    def _():
        cond[0:WIDE] = jnp.zeros((WIDE, cr + 2 * ROWS, lanes), jnp.float32)

    @pl.when(layer == layers - 1)
    def _():
        cond[WIDE + ca :] = jnp.zeros((WIDE, cr + 2 * ROWS, lanes), jnp.float32)

    own_src.wait()
    halo_all(0, src, source, False)
    halo_all(1, cond, None, False)

    def inside(e, values):
        at = layer * ca + e - WIDE
        return jnp.where(jnp.logical_and(at >= 0, at < layers * ca), values, 0.0)

    ratio = THETA / DELTA
    rho = [1.0 / ratio]
    for _ in range(2):
        rho.append(1.0 / (2.0 * ratio - rho[-1]))

    def first(e, carry):
        here, others = around(cond, e)
        diag = 0.5 * (here + others[0])
        for other in others[1:]:
            diag = diag + 0.5 * (here + other)
        inverse = 1.0 / diag
        inv[e] = inverse
        dir_a[e] = inside(e, inverse * src[e] / THETA)
        return carry

    lax.fori_loop(1, 2 * WIDE + ca - 1, first, 0)

    def operate(field, e):
        here, others = around(cond, e)
        v, vs = around(field, e)
        result = 0.5 * (here + others[0]) * (v - vs[0])
        for other, other_v in zip(others[1:], vs[1:]):
            result = result + 0.5 * (here + other) * (v - other_v)
        return v, result

    def second(e, carry):
        v, applied = operate(dir_a, e)
        left = src[e] - applied
        res[e] = left
        step = inside(e, (rho[1] * rho[0]) * v + (2.0 * rho[1] / DELTA) * (inv[e] * left))
        dir_b[e] = step
        pot[e] = v + step
        return carry

    lax.fori_loop(2, 2 * WIDE + ca - 2, second, 0)

    def third(e, carry):
        v, applied = operate(dir_b, e)
        left = res[e] - applied
        step = inside(e, (rho[2] * rho[1]) * v + (2.0 * rho[2] / DELTA) * (inv[e] * left))
        pot[e] = pot[e] + step
        return carry

    lax.fori_loop(3, 2 * WIDE + ca - 3, third, 0)

    def joule(a, total):
        v, others = around(pot, a + WIDE)
        result = jnp.zeros_like(v)
        for other in others:
            gap = v - other
            result = result + 0.5 * gap * gap
        result = cond[a + WIDE] * result
        power[pl.ds(pl.multiple_of(a * cr, 8), cr), :] = result[ROWS : ROWS + cr]
        potential[a] = v[ROWS : ROWS + cr]
        return total + jnp.sum(result[ROWS : ROWS + cr], axis=0, keepdims=True)

    part[...] = lax.fori_loop(0, ca, joule, jnp.zeros((1, lanes), jnp.float32))
    sums[me] = part[...]

    def pow_copy(j, slot):
        return remote(
            rows.at[pl.ds(pl.multiple_of(j * cap, 8), cap)],
            arrived.at[pl.ds(pl.multiple_of(slot * cap, 8), cap)],
            pow_send.at[j], pow_recv.at[slot], j,
        )

    def sum_copy(j, slot):
        return remote(part, sums.at[slot], sum_send.at[j], sum_recv.at[slot], j)

    def send_power(k, carry):
        j = lax.rem(me + k, n)
        base = pl.multiple_of(j * cap, 8)

        @pl.when(k < n)
        def _():
            row_copy(j, me).wait_send()
            fill(rows, base, lambda c: blocks[j, c], lambda i: power[pl.ds(i, 1), :])
            pow_copy(j, me).start()
            sum_copy(j, me).start()

        @pl.when(k == n)
        def _():
            fill(arrived, base, lambda c: blocks[j, c], lambda i: power[pl.ds(i, 1), :])

        return carry

    lax.fori_loop(1, n + 1, send_power, 0)

    def finish(k, carry):
        j = lax.rem(me + k, n)
        ask_copy(j, j).wait_send()
        pow_copy(j, j).wait()
        sum_copy(j, j).wait()
        return carry

    lax.fori_loop(1, n, finish, 0)


def thermal_kernel(scale, wanted, arrived, sums, temp_old, heat_cap, conduct, temp_new, heat):
    n, cap = wanted.shape
    count = temp_old.shape[0]
    factor = scale / jnp.sum(sums[...])

    def land(j, carry):
        for c in range(cap):
            heat[pl.ds(wanted[j, c] + 7, 1), :] = arrived[pl.ds(j * cap + c, 1), :]
        return carry

    lax.fori_loop(0, n, land, 0)
    step = 64

    def solve(b, carry):
        at = pl.ds(pl.multiple_of(b * step, 8), step)
        k = conduct[at, :]
        left = 0.5 * (k + shifted(k, 1, 1, False))
        right = 0.5 * (k + shifted(k, -1, 1, False))
        lane = lax.broadcasted_iota(jnp.int32, k.shape, 1)
        left = jnp.where(lane == 0, 0.0, left)
        right = jnp.where(lane == k.shape[1] - 1, 0.0, right)
        cap_here = heat_cap[at, :]
        total = cap_here + left + right
        old = temp_old[at, :]
        target = cap_here * old + heat[pl.ds(pl.multiple_of(b * step + 8, 8), step), :] * factor
        current = old
        for _ in range(JACOBI):
            before = shifted(current, 1, 1, True)
            after = shifted(current, -1, 1, True)
            current = (target + left * before + right * after) / total
        temp_new[at, :] = current
        return carry

    lax.fori_loop(0, count // step, solve, 0)


def per_device(source, sigma_ref, owner, slot, temp_old, heat_cap, conduct):
    layers, blks = lax.axis_size("layer"), lax.axis_size("blk")
    peers = layers * blks
    ca, cr, lanes = source.shape
    count = temp_old.shape[0]
    positions, slot_code, block_code = routing(owner, slot, peers)
    cap = slot_code.shape[1]
    ask = jnp.pad(slot_code, ((0, 0), (0, 128 - cap)))[:, None, :]
    ext = pltpu.VMEM((ca + 2 * WIDE, cr + 2 * ROWS, lanes), jnp.float32)
    vmem, smem = pl.BlockSpec(memory_space=pltpu.VMEM), pl.BlockSpec(memory_space=pltpu.SMEM)
    each = pltpu.SemaphoreType.DMA((peers,))

    def kernel(*refs):
        exchange_kernel(layers, blks, ca, *refs)

    potential, arrived, wanted, sums = pl.pallas_call(
        kernel,
        out_shape=(
            jax.ShapeDtypeStruct(source.shape, jnp.float32),
            jax.ShapeDtypeStruct((peers * cap, lanes), jnp.float32),
            jax.ShapeDtypeStruct((peers, 1, 128), jnp.int32),
            jax.ShapeDtypeStruct((peers, 1, lanes), jnp.float32),
        ),
        in_specs=[vmem] * 4 + [smem] * 2,
        out_specs=(vmem,) * 4,
        scratch_shapes=[
            pltpu.SMEM((peers, 1, 128), jnp.int32),
            pltpu.VMEM((peers * cap, lanes), jnp.float32),
            pltpu.VMEM((peers * cap, lanes), jnp.float32),
            ext, ext, ext, ext, ext, ext, ext,
            pltpu.VMEM((ca * cr, lanes), jnp.float32),
            pltpu.VMEM((1, lanes), jnp.float32),
            pltpu.SemaphoreType.DMA((3,)),
            each, each, each, each, each, each, each, each,
            pltpu.SemaphoreType.DMA((2, 8)),
            pltpu.SemaphoreType.DMA((2, 8)),
        ],
        compiler_params=pltpu.CompilerParams(
            collective_id=0, has_side_effects=True, vmem_limit_bytes=40 << 20
        ),
    )(source, sigma_ref, temp_old, ask, positions.reshape(ca, cr), block_code)
    scale = source.size * peers

    def heat_step(*refs):
        thermal_kernel(float(scale), *refs)

    temp_new = pl.pallas_call(
        heat_step,
        out_shape=jax.ShapeDtypeStruct(temp_old.shape, jnp.float32),
        in_specs=[smem] + [vmem] * 5,
        out_specs=vmem,
        scratch_shapes=[pltpu.VMEM((count + 8, lanes), jnp.float32)],
        compiler_params=pltpu.CompilerParams(vmem_limit_bytes=40 << 20),
    )(wanted[:, 0, :cap], arrived, sums, temp_old, heat_cap, conduct)
    return (potential, temp_new)


def solution(mesh):
    return jax.shard_map(
        per_device,
        mesh=mesh,
        in_specs=(
            P("layer", "blk", None),
            P("layer", "blk", None),
            P("layer", "blk"),
            P("layer", "blk"),
            P(("blk", "layer"), None),
            P(("blk", "layer"), None),
            P(("blk", "layer"), None),
        ),
        out_specs=(P("layer", "blk", None), P(("blk", "layer"), None)),
        check_vma=False,
    )
```

time: 173 us -> 94.9 us (0.55)
  the two profiles are of different devices: /device:TPU:1 before, /device:TPU:15 now
where the time goes in v2:
time: 94.9 us; the launch traced here: 94.7 us
  Pallas kernels  89.2 us (94%)
  local copies, waits for them, and re-layouts  2.67 us (3%)
  other arithmetic  1.02 us (1%)
  matrix products  1.01 us (1%)
    pallas_call x1, Pallas kernels, per_device(): pl.pallas_call(kernel, out_shape=(jax.ShapeDtypeStruct(source.shape, jnp....  82.7 us
    pallas_call x1, Pallas kernels, per_device(): pl.pallas_call(heat_step, out_shape=jax.ShapeDtypeStruct(temp_old.shape,...  6.52 us

profile of v2, /device:TPU:15, one launch (start us, length us, event | category | flops | bytes accessed | tf_op | source)
XLA Modules:
  0.0 94.7 jit_solution(3638629325328996141)
XLA Ops:
  0.6 0.0 copy-start.5
  0.6 0.0 copy-start.6
  0.6 0.8 eq.28
  1.5 0.5 fusion.2
  2.0 0.1 convert_element_type.63
  2.1 0.0 copy-done.5
  2.1 0.0 copy-done.6
  2.1 0.1 convert_element_type.57
  2.2 0.1 convert_element_type.59
  2.3 1.0 %select_convert_fusion.3 = (bf16[1024,64]{1,0:T(8,128)(2,1)S(1)}, bf16[1024,64]{1,0:T(8,128)(2,1)S(1)}, bf16[1024,64]{1,0:T(8,128)(2,1)S(1)}, bf16[1024,64]{1,0:T(8,128)(2,1)S(1)}) fusion(bf16[1024]{0:T(1024)(128)(2,1)S(1)} %convert_element_type.57, s32[1024]{0:T(1024)S(1)} %convert_element_type.55, bf16[1024]{0:T(1024)(128)(2,1)S(1)} %get-tuple-element.20, ...), kind=kLoop, calls=%fused_computation.15 | loop fusion | flops 327680 | bytes 536576 | tf_op jit(solution)/shard_map/convert
  3.3 0.0 copy-start
  3.3 0.0 copy-start.1
  3.3 0.0 copy-start.2
  3.3 0.5 convolution_convert_fusion
  3.8 0.0 copy-start.3
  3.8 0.0 copy-start.4
  3.8 0.1 reshape.56
  4.0 0.3 copy-done
  4.3 0.2 copy-done.1
  4.5 0.2 copy-done.2
  4.7 82.7 %shard_map.86 = (f32[16,64,128]{2,1,0:T(8,128)S(1)}, f32[2048,128]{1,0:T(8,128)S(1)}, s32[32,1,128]{2,1,0:T(1,128)S(1)}, f32[32,1,128]{2,1,0:T(1,128)S(1)}) custom-call(f32[16,64,128]{2,1,0:T(8,128)S(1)} %copy-done.1, f32[16,64,128]{2,1,0:T(8,128)S(1)} %copy-done.2, f32[1024,128]{1,0:T(8,128)S(1)} %copy-done, s32[32,1,128]{2,1,0:T(1,128)S(1)} %bitcast.14, ...), custom_call_target="tpu_custom_call" | custom-call | tf_op jit(solution)/shard_map/pallas_call | solution.py:380
  87.3 0.0 copy-done.3
  87.4 6.5 %shard_map.87 = f32[1024,128]{1,0:T(8,128)} custom-call(s32[32,64]{1,0:T(8,128)S(1)} %slice_bitcast_fusion.refs_0_, f32[2048,128]{1,0:T(8,128)S(1)} %get-tuple-element.8.refs_1_, f32[32,1,128]{2,1,0:T(1,128)S(1)} %get-tuple-element.9.refs_2_, f32[1024,128]{1,0:T(8,128)S(1)} %copy-done, f32[1024,128]{1,0:T(8,128)S(1)} %copy-done.3, f32[1024,128]{1,0:T(8,128)S(1)} %copy-done.4), custom_call_target="tpu_custom_call" | custom-call | tf_op jit(solution)/shard_map/pallas_call | solution.py:411
  93.9 0.8 copy.22
  (10 shorter events, 0.1 us)
Async XLA Ops:
  0.6 1.5 %copy-start.5 = (s32[16,64]{1,0:T(8,128)S(1)}, s32[16,64]{1,0:T(8,128)}, u32[]{:S(2)}) copy-start(s32[16,64]{1,0:T(8,128)} %param.9) | copy-start | bytes 12292
  0.6 1.5 %copy-start.6 = (s32[16,64]{1,0:T(8,128)S(1)}, s32[16,64]{1,0:T(8,128)}, u32[]{:S(2)}) copy-start(s32[16,64]{1,0:T(8,128)} %param.10) | copy-start | bytes 12292
  3.3 1.0 %copy-start = (f32[1024,128]{1,0:T(8,128)S(1)}, f32[1024,128]{1,0:T(8,128)}, u32[]{:S(2)}) copy-start(f32[1024,128]{1,0:T(8,128)} %refs_3_.1) | copy-start | bytes 1572868
  3.3 1.2 %copy-start.1 = (f32[16,64,128]{2,1,0:T(8,128)S(1)}, f32[16,64,128]{2,1,0:T(8,128)}, u32[]{:S(2)}) copy-start(f32[16,64,128]{2,1,0:T(8,128)} %refs_0_.1) | copy-start | bytes 1572868
  3.3 1.3 %copy-start.2 = (f32[16,64,128]{2,1,0:T(8,128)S(1)}, f32[16,64,128]{2,1,0:T(8,128)}, u32[]{:S(2)}) copy-start(f32[16,64,128]{2,1,0:T(8,128)} %refs_1_.1) | copy-start | bytes 1572868
  3.8 83.5 %copy-start.3 = (f32[1024,128]{1,0:T(8,128)S(1)}, f32[1024,128]{1,0:T(8,128)}, u32[]{:S(2)}) copy-start(f32[1024,128]{1,0:T(8,128)} %refs_4_.1) | copy-start | bytes 1572868
  3.8 83.5 %copy-start.4 = (f32[1024,128]{1,0:T(8,128)S(1)}, f32[1024,128]{1,0:T(8,128)}, u32[]{:S(2)}) copy-start(f32[1024,128]{1,0:T(8,128)} %refs_5_.1) | copy-start | bytes 1572868

commit v3 on v2

--- a/solution.py
+++ b/solution.py
@@ -79,18 +79,37 @@
     blk, layer = lax.axis_index("blk"), lax.axis_index("layer")
     me = blk * layers + layer
 
-    def peer(j):
-        return (j // layers, j % layers)
+    def wrap(x, size):
+        return jnp.where(x >= size, x - size, jnp.where(x < 0, x + size, x))
+
+    def others(body, sign):
+        def outer(kl, carry):
+            to_layer = wrap(layer + sign * kl, layers)
+
+            def inner(pair, carry):
+                for start in (blks // 2, 0):
+                    to_blk = wrap(blk + sign * (pair + start), blks)
+                    j = to_blk * layers + to_layer
+
+                    def go(to_blk=to_blk, j=j):
+                        body((to_blk, to_layer), j)
+
+                    if start:
+                        go()
+                    else:
+                        pl.when(jnp.logical_or(pair > 0, kl > 0))(go)
+                return carry
+
+            return lax.fori_loop(0, blks // 2, inner, carry)
+
+        lax.fori_loop(0, layers, outer, 0)
 
     barrier = pltpu.get_barrier_semaphore()
 
-    def greet(k, carry):
-        pl.semaphore_signal(
-            barrier, inc=1, device_id=peer(lax.rem(me + k, n)), device_id_type=MESH
-        )
-        return carry
-
-    lax.fori_loop(1, n, greet, 0)
+    def greet(at, j):
+        pl.semaphore_signal(barrier, inc=1, device_id=at, device_id_type=MESH)
+
+    others(greet, 1)
     own_src = pltpu.make_async_copy(
         source, src.at[pl.ds(WIDE, ca), pl.ds(ROWS, cr)], local_sem.at[0]
     )
@@ -99,20 +118,16 @@
     own_ask.start()
     pl.semaphore_wait(barrier, n - 1)
 
-    def remote(src_ref, dst_ref, send, recv, j):
+    def remote(src_ref, dst_ref, send, recv, at):
         return pltpu.make_async_remote_copy(
             src_ref=src_ref, dst_ref=dst_ref, send_sem=send, recv_sem=recv,
-            device_id=peer(j), device_id_type=MESH,
+            device_id=at, device_id_type=MESH,
         )
 
-    def ask_copy(j, slot):
-        return remote(ask.at[j], wanted.at[slot], ask_send.at[j], ask_recv.at[slot], j)
-
-    def send_ask(k, carry):
-        ask_copy(lax.rem(me + k, n), me).start()
-        return carry
-
-    lax.fori_loop(1, n, send_ask, 0)
+    def ask_copy(at, j, slot):
+        return remote(ask.at[j], wanted.at[slot], ask_send.at[j], ask_recv.at[slot], at)
+
+    others(lambda at, j: ask_copy(at, j, me).start(), -1)
 
     directions = [(a, r) for a in (-1, 0, 1) for r in (-1, 0, 1) if (a, r) != (0, 0)]
 
@@ -159,48 +174,32 @@
     halo_all(0, src, source, True)
     own_ask.wait()
 
-    def row_copy(j, slot):
+    def row_copy(at, j, slot):
         return remote(
             rows.at[pl.ds(pl.multiple_of(j * cap, 8), cap)],
             fetched.at[pl.ds(pl.multiple_of(slot * cap, 8), cap)],
-            row_send.at[j], row_recv.at[slot], j,
+            row_send.at[j], row_recv.at[slot], at,
         )
 
     def fill(target, base, table, get):
         for c in range(cap):
             target[pl.ds(base + c, 1), :] = get(jnp.maximum(table(c) - 1, 0))
 
-    def reply(k, carry):
-        j = lax.rem(me - k + n, n)
-
-        @pl.when(k > 0)
-        def _():
-            ask_copy(j, j).wait_recv()
-
-        to_scalar = pltpu.make_async_copy(wanted.at[j], asked.at[j], local_sem.at[2])
-        to_scalar.start()
-        to_scalar.wait()
-        base = pl.multiple_of(j * cap, 8)
-
-        @pl.when(k > 0)
-        def _():
-            fill(rows, base, lambda c: asked[j, 0, c], lambda i: temp_old[pl.ds(i, 1), :])
-            row_copy(j, me).start()
-
-        @pl.when(k == 0)
-        def _():
-            fill(fetched, base, lambda c: asked[j, 0, c], lambda i: temp_old[pl.ds(i, 1), :])
-
-        return carry
-
-    lax.fori_loop(0, n, reply, 0)
-
-    def got_row(k, carry):
-        j = lax.rem(me + k, n)
-        row_copy(j, j).wait_recv()
-        return carry
-
-    lax.fori_loop(1, n, got_row, 0)
+    others(lambda at, j: ask_copy(at, j, j).wait_recv(), 1)
+    to_scalar = pltpu.make_async_copy(wanted, asked, local_sem.at[2])
+    to_scalar.start()
+    to_scalar.wait()
+
+    def old_row(i):
+        return temp_old[pl.ds(i, 1), :]
+
+    def reply(at, j):
+        fill(rows, pl.multiple_of(j * cap, 8), lambda c: asked[j, 0, c], old_row)
+        row_copy(at, j, me).start()
+
+    others(reply, 1)
+    fill(fetched, pl.multiple_of(me * cap, 8), lambda c: asked[me, 0, c], old_row)
+    others(lambda at, j: row_copy(at, j, j).wait_recv(), -1)
 
     def place(a, carry):
         for r in range(cr):
@@ -287,53 +286,53 @@
     part[...] = lax.fori_loop(0, ca, joule, jnp.zeros((1, lanes), jnp.float32))
     sums[me] = part[...]
 
-    def pow_copy(j, slot):
+    def pow_copy(at, j, slot):
         return remote(
             rows.at[pl.ds(pl.multiple_of(j * cap, 8), cap)],
             arrived.at[pl.ds(pl.multiple_of(slot * cap, 8), cap)],
-            pow_send.at[j], pow_recv.at[slot], j,
+            pow_send.at[j], pow_recv.at[slot], at,
         )
 
-    def sum_copy(j, slot):
-        return remote(part, sums.at[slot], sum_send.at[j], sum_recv.at[slot], j)
-
-    def send_power(k, carry):
-        j = lax.rem(me + k, n)
-        base = pl.multiple_of(j * cap, 8)
-
-        @pl.when(k < n)
-        def _():
-            row_copy(j, me).wait_send()
-            fill(rows, base, lambda c: blocks[j, c], lambda i: power[pl.ds(i, 1), :])
-            pow_copy(j, me).start()
-            sum_copy(j, me).start()
-
-        @pl.when(k == n)
-        def _():
-            fill(arrived, base, lambda c: blocks[j, c], lambda i: power[pl.ds(i, 1), :])
-
-        return carry
-
-    lax.fori_loop(1, n + 1, send_power, 0)
-
-    def finish(k, carry):
-        j = lax.rem(me + k, n)
-        ask_copy(j, j).wait_send()
-        pow_copy(j, j).wait()
-        sum_copy(j, j).wait()
-        return carry
-
-    lax.fori_loop(1, n, finish, 0)
-
-
-def thermal_kernel(scale, wanted, arrived, sums, temp_old, heat_cap, conduct, temp_new, heat):
+    def sum_copy(at, j, slot):
+        return remote(part, sums.at[slot], sum_send.at[j], sum_recv.at[slot], at)
+
+    def power_row(i):
+        return power[pl.ds(i, 1), :]
+
+    def send_power(at, j):
+        row_copy(at, j, me).wait_send()
+        fill(rows, pl.multiple_of(j * cap, 8), lambda c: blocks[j, c], power_row)
+        pow_copy(at, j, me).start()
+        sum_copy(at, j, me).start()
+
+    others(send_power, 1)
+    fill(arrived, pl.multiple_of(me * cap, 8), lambda c: blocks[me, c], power_row)
+
+    def finish(at, j):
+        ask_copy(at, j, j).wait_send()
+        pow_copy(at, j, j).wait()
+        sum_copy(at, j, j).wait()
+
+    others(finish, -1)
+
+
+def thermal_kernel(
+    scale, wanted, potential_in, arrived, sums, temp_old, heat_cap, conduct,
+    temp_new, potential, heat, sem,
+):
+    through = pltpu.make_async_copy(potential_in, potential, sem)
+    through.start()
     n, cap = wanted.shape
     count = temp_old.shape[0]
     factor = scale / jnp.sum(sums[...])
 
     def land(j, carry):
-        for c in range(cap):
-            heat[pl.ds(wanted[j, c] + 7, 1), :] = arrived[pl.ds(j * cap + c, 1), :]
+        for group in range(0, cap, 8):
+            @pl.when(wanted[j, group] > 0)
+            def _(group=group):
+                for c in range(group, group + 8):
+                    heat[pl.ds(wanted[j, c] + 7, 1), :] = arrived[pl.ds(j * cap + c, 1), :]
+
         return carry
 
     lax.fori_loop(0, n, land, 0)
@@ -360,6 +359,7 @@
         return carry
 
     lax.fori_loop(0, count // step, solve, 0)
+    through.wait()
 
 
 def per_device(source, sigma_ref, owner, slot, temp_old, heat_cap, conduct):
@@ -408,14 +408,21 @@
     def heat_step(*refs):
         thermal_kernel(float(scale), *refs)
 
-    temp_new = pl.pallas_call(
+    whole = pl.BlockSpec(memory_space=pl.ANY)
+    temp_new, potential = pl.pallas_call(
         heat_step,
-        out_shape=jax.ShapeDtypeStruct(temp_old.shape, jnp.float32),
-        in_specs=[smem] + [vmem] * 5,
-        out_specs=vmem,
-        scratch_shapes=[pltpu.VMEM((count + 8, lanes), jnp.float32)],
+        out_shape=(
+            jax.ShapeDtypeStruct(temp_old.shape, jnp.float32),
+            jax.ShapeDtypeStruct(source.shape, jnp.float32),
+        ),
+        in_specs=[smem, whole] + [vmem] * 5,
+        out_specs=(vmem, whole),
+        scratch_shapes=[
+            pltpu.VMEM((count + 8, lanes), jnp.float32),
+            pltpu.SemaphoreType.DMA(()),
+        ],
         compiler_params=pltpu.CompilerParams(vmem_limit_bytes=40 << 20),
-    )(wanted[:, 0, :cap], arrived, sums, temp_old, heat_cap, conduct)
+    )(wanted[:, 0, :cap], potential, arrived, sums, temp_old, heat_cap, conduct)
     return (potential, temp_new)
 
 

time: 94.9 us -> 92.5 us (0.975)
  the two profiles are of different devices: /device:TPU:15 before, /device:TPU:1 now
where the time goes in v3:
time: 92.5 us; the launch traced here: 92.3 us
  Pallas kernels  87.6 us (95%)
  local copies, waits for them, and re-layouts  1.87 us (2%)
  other arithmetic  1.02 us (1%)
  matrix products  1 us (1%)
    pallas_call x1, Pallas kernels, per_device(): pl.pallas_call(kernel, out_shape=(jax.ShapeDtypeStruct(source.shape, jnp....  79.8 us
    pallas_call x1, Pallas kernels, per_device(): pl.pallas_call(heat_step, out_shape=(jax.ShapeDtypeStruct(temp_old.shape,...  7.82 us

profile of v3, /device:TPU:1, one launch (start us, length us, event | category | flops | bytes accessed | tf_op | source)
XLA Modules:
  0.0 92.3 jit_solution(5879292986410388802)
XLA Ops:
  0.6 0.0 copy-start.5
  0.6 0.0 copy-start.6
  0.6 0.8 eq.28
  1.5 0.5 fusion.2
  2.0 0.1 convert_element_type.63
  2.1 0.0 copy-done.5
  2.1 0.0 copy-done.6
  2.1 0.1 convert_element_type.57
  2.2 0.1 convert_element_type.59
  2.3 1.0 %select_convert_fusion.3 = (bf16[1024,64]{1,0:T(8,128)(2,1)S(1)}, bf16[1024,64]{1,0:T(8,128)(2,1)S(1)}, bf16[1024,64]{1,0:T(8,128)(2,1)S(1)}, bf16[1024,64]{1,0:T(8,128)(2,1)S(1)}) fusion(bf16[1024]{0:T(1024)(128)(2,1)S(1)} %convert_element_type.57, s32[1024]{0:T(1024)S(1)} %convert_element_type.55, bf16[1024]{0:T(1024)(128)(2,1)S(1)} %get-tuple-element.24, ...), kind=kLoop, calls=%fused_computation.15 | loop fusion | flops 327680 | bytes 536576 | tf_op jit(solution)/shard_map/convert
  3.3 0.0 copy-start
  3.3 0.0 copy-start.1
  3.3 0.0 copy-start.2
  3.3 0.5 convolution_convert_fusion
  3.8 0.0 copy-start.3
  3.8 0.0 copy-start.4
  3.8 0.1 reshape.56
  4.0 0.3 copy-done
  4.3 0.2 copy-done.1
  4.5 0.2 copy-done.2
  4.7 79.8 %shard_map.86 = (f32[16,64,128]{2,1,0:T(8,128)S(1)}, f32[2048,128]{1,0:T(8,128)S(1)}, s32[32,1,128]{2,1,0:T(1,128)S(1)}, f32[32,1,128]{2,1,0:T(1,128)S(1)}) custom-call(f32[16,64,128]{2,1,0:T(8,128)S(1)} %copy-done.1, f32[16,64,128]{2,1,0:T(8,128)S(1)} %copy-done.2, f32[1024,128]{1,0:T(8,128)S(1)} %copy-done, s32[32,1,128]{2,1,0:T(1,128)S(1)} %bitcast.14, ...), custom_call_target="tpu_custom_call" | custom-call | tf_op jit(solution)/shard_map/pallas_call | solution.py:380
  84.4 0.0 copy-done.3
  84.4 0.0 copy-done.4
  84.5 7.8 %shard_map.87 = (f32[1024,128]{1,0:T(8,128)}, f32[16,64,128]{2,1,0:T(8,128)}) custom-call(s32[32,64]{1,0:T(8,128)S(1)} %slice_bitcast_fusion.refs_0_, f32[16,64,128]{2,1,0:T(8,128)S(1)} %get-tuple-element.9.refs_1_, f32[2048,128]{1,0:T(8,128)S(1)} %get-tuple-element.10.refs_2_, f32[32,1,128]{2,1,0:T(1,128)S(1)} %get-tuple-element.11.refs_3_, ...), custom_call_target="tpu_custom_call" | custom-call | tf_op jit(solution)/shard_map/pallas_call | solution.py:412
  (9 shorter events, 0.1 us)
Async XLA Ops:
  0.6 1.5 %copy-start.5 = (s32[16,64]{1,0:T(8,128)S(1)}, s32[16,64]{1,0:T(8,128)}, u32[]{:S(2)}) copy-start(s32[16,64]{1,0:T(8,128)} %param.9) | copy-start | bytes 12292
  0.6 1.5 %copy-start.6 = (s32[16,64]{1,0:T(8,128)S(1)}, s32[16,64]{1,0:T(8,128)}, u32[]{:S(2)}) copy-start(s32[16,64]{1,0:T(8,128)} %param.10) | copy-start | bytes 12292
  3.3 1.0 %copy-start = (f32[1024,128]{1,0:T(8,128)S(1)}, f32[1024,128]{1,0:T(8,128)}, u32[]{:S(2)}) copy-start(f32[1024,128]{1,0:T(8,128)} %refs_4_.1) | copy-start | bytes 1572868
  3.3 1.2 %copy-start.1 = (f32[16,64,128]{2,1,0:T(8,128)S(1)}, f32[16,64,128]{2,1,0:T(8,128)}, u32[]{:S(2)}) copy-start(f32[16,64,128]{2,1,0:T(8,128)} %refs_0_.1) | copy-start | bytes 1572868
  3.3 1.3 %copy-start.2 = (f32[16,64,128]{2,1,0:T(8,128)S(1)}, f32[16,64,128]{2,1,0:T(8,128)}, u32[]{:S(2)}) copy-start(f32[16,64,128]{2,1,0:T(8,128)} %refs_1_.1) | copy-start | bytes 1572868
  3.8 80.6 %copy-start.3 = (f32[1024,128]{1,0:T(8,128)S(1)}, f32[1024,128]{1,0:T(8,128)}, u32[]{:S(2)}) copy-start(f32[1024,128]{1,0:T(8,128)} %refs_5_.1) | copy-start | bytes 1572868
  3.8 80.6 %copy-start.4 = (f32[1024,128]{1,0:T(8,128)S(1)}, f32[1024,128]{1,0:T(8,128)}, u32[]{:S(2)}) copy-start(f32[1024,128]{1,0:T(8,128)} %refs_6_.1) | copy-start | bytes 1572868

commit v4 on v3

--- a/solution.py
+++ b/solution.py
@@ -242,7 +242,7 @@
         dir_a[e] = inside(e, inverse * src[e] / THETA)
         return carry
 
-    lax.fori_loop(1, 2 * WIDE + ca - 1, first, 0)
+    lax.fori_loop(1, 2 * WIDE + ca - 1, first, 0, unroll=2)
 
     def operate(field, e):
         here, others = around(cond, e)
@@ -261,7 +261,7 @@
         pot[e] = v + step
         return carry
 
-    lax.fori_loop(2, 2 * WIDE + ca - 2, second, 0)
+    lax.fori_loop(2, 2 * WIDE + ca - 2, second, 0, unroll=2)
 
     def third(e, carry):
         v, applied = operate(dir_b, e)
@@ -270,7 +270,7 @@
         pot[e] = pot[e] + step
         return carry
 
-    lax.fori_loop(3, 2 * WIDE + ca - 3, third, 0)
+    lax.fori_loop(3, 2 * WIDE + ca - 3, third, 0, unroll=2)
 
     def joule(a, total):
         v, others = around(pot, a + WIDE)
@@ -327,16 +327,12 @@
     factor = scale / jnp.sum(sums[...])
 
     def land(j, carry):
-        for group in range(0, cap, 8):
-            @pl.when(wanted[j, group] > 0)
-            def _(group=group):
-                for c in range(group, group + 8):
-                    heat[pl.ds(wanted[j, c] + 7, 1), :] = arrived[pl.ds(j * cap + c, 1), :]
-
+        for c in range(cap):
+            heat[pl.ds(wanted[j, c] + 7, 1), :] = arrived[pl.ds(j * cap + c, 1), :]
         return carry
 
     lax.fori_loop(0, n, land, 0)
-    step = 64
+    step = 128
 
     def solve(b, carry):
         at = pl.ds(pl.multiple_of(b * step, 8), step)

time: 92.5 us -> 87.8 us (0.949)
  Pallas kernels: 87.6 us -> 82.9 us
    pallas_call x1, Pallas kernels: 7.82 us -> 5.39 us  [per_device(): pl.pallas_call(heat_step, out_shape=(jax.ShapeDtypeStruct(temp_old.shape,...]
    pallas_call x1, Pallas kernels: 79.8 us -> 77.5 us  [per_device(): pl.pallas_call(kernel, out_shape=(jax.ShapeDtypeStruct(source.shape, jnp....]
where the time goes in v4:
time: 87.8 us; the launch traced here: 87.6 us
  Pallas kernels  82.9 us (94%)
  local copies, waits for them, and re-layouts  1.87 us (2%)
  other arithmetic  1.02 us (1%)
  matrix products  1 us (1%)
    pallas_call x1, Pallas kernels, per_device(): pl.pallas_call(kernel, out_shape=(jax.ShapeDtypeStruct(source.shape, jnp....  77.5 us
    pallas_call x1, Pallas kernels, per_device(): pl.pallas_call(heat_step, out_shape=(jax.ShapeDtypeStruct(temp_old.shape,...  5.39 us

profile of v4, /device:TPU:1, one launch (start us, length us, event | category | flops | bytes accessed | tf_op | source)
XLA Modules:
  0.0 87.6 jit_solution(12305090623715792831)
XLA Ops:
  0.6 0.0 copy-start.5
  0.6 0.0 copy-start.6
  0.6 0.8 eq.28
  1.5 0.5 fusion.2
  2.0 0.1 convert_element_type.63
  2.1 0.0 copy-done.5
  2.1 0.0 copy-done.6
  2.1 0.1 convert_element_type.57
  2.2 0.1 convert_element_type.59
  2.3 1.0 %select_convert_fusion.3 = (bf16[1024,64]{1,0:T(8,128)(2,1)S(1)}, bf16[1024,64]{1,0:T(8,128)(2,1)S(1)}, bf16[1024,64]{1,0:T(8,128)(2,1)S(1)}, bf16[1024,64]{1,0:T(8,128)(2,1)S(1)}) fusion(bf16[1024]{0:T(1024)(128)(2,1)S(1)} %convert_element_type.57, s32[1024]{0:T(1024)S(1)} %convert_element_type.55, bf16[1024]{0:T(1024)(128)(2,1)S(1)} %get-tuple-element.24, ...), kind=kLoop, calls=%fused_computation.15 | loop fusion | flops 327680 | bytes 536576 | tf_op jit(solution)/shard_map/convert
  3.3 0.0 copy-start
  3.3 0.0 copy-start.1
  3.3 0.0 copy-start.2
  3.3 0.5 convolution_convert_fusion
  3.8 0.0 copy-start.3
  3.8 0.0 copy-start.4
  3.8 0.1 reshape.56
  4.0 0.3 copy-done
  4.3 0.2 copy-done.1
  4.5 0.2 copy-done.2
  4.7 77.5 %shard_map.86 = (f32[16,64,128]{2,1,0:T(8,128)S(1)}, f32[2048,128]{1,0:T(8,128)S(1)}, s32[32,1,128]{2,1,0:T(1,128)S(1)}, f32[32,1,128]{2,1,0:T(1,128)S(1)}) custom-call(f32[16,64,128]{2,1,0:T(8,128)S(1)} %copy-done.1, f32[16,64,128]{2,1,0:T(8,128)S(1)} %copy-done.2, f32[1024,128]{1,0:T(8,128)S(1)} %copy-done, s32[32,1,128]{2,1,0:T(1,128)S(1)} %bitcast.14, ...), custom_call_target="tpu_custom_call" | custom-call | tf_op jit(solution)/shard_map/pallas_call | solution.py:376
  82.2 0.0 copy-done.3
  82.2 0.0 copy-done.4
  82.2 5.4 %shard_map.87 = (f32[1024,128]{1,0:T(8,128)}, f32[16,64,128]{2,1,0:T(8,128)}) custom-call(s32[32,64]{1,0:T(8,128)S(1)} %slice_bitcast_fusion.refs_0_, f32[16,64,128]{2,1,0:T(8,128)S(1)} %get-tuple-element.9.refs_1_, f32[2048,128]{1,0:T(8,128)S(1)} %get-tuple-element.10.refs_2_, f32[32,1,128]{2,1,0:T(1,128)S(1)} %get-tuple-element.11.refs_3_, ...), custom_call_target="tpu_custom_call" | custom-call | tf_op jit(solution)/shard_map/pallas_call | solution.py:408
  (9 shorter events, 0.1 us)
Async XLA Ops:
  0.6 1.5 %copy-start.5 = (s32[16,64]{1,0:T(8,128)S(1)}, s32[16,64]{1,0:T(8,128)}, u32[]{:S(2)}) copy-start(s32[16,64]{1,0:T(8,128)} %param.9) | copy-start | bytes 12292
  0.6 1.5 %copy-start.6 = (s32[16,64]{1,0:T(8,128)S(1)}, s32[16,64]{1,0:T(8,128)}, u32[]{:S(2)}) copy-start(s32[16,64]{1,0:T(8,128)} %param.10) | copy-start | bytes 12292
  3.3 1.0 %copy-start = (f32[1024,128]{1,0:T(8,128)S(1)}, f32[1024,128]{1,0:T(8,128)}, u32[]{:S(2)}) copy-start(f32[1024,128]{1,0:T(8,128)} %refs_4_.1) | copy-start | bytes 1572868
  3.3 1.2 %copy-start.1 = (f32[16,64,128]{2,1,0:T(8,128)S(1)}, f32[16,64,128]{2,1,0:T(8,128)}, u32[]{:S(2)}) copy-start(f32[16,64,128]{2,1,0:T(8,128)} %refs_0_.1) | copy-start | bytes 1572868
  3.3 1.3 %copy-start.2 = (f32[16,64,128]{2,1,0:T(8,128)S(1)}, f32[16,64,128]{2,1,0:T(8,128)}, u32[]{:S(2)}) copy-start(f32[16,64,128]{2,1,0:T(8,128)} %refs_1_.1) | copy-start | bytes 1572868
  3.8 78.4 %copy-start.3 = (f32[1024,128]{1,0:T(8,128)S(1)}, f32[1024,128]{1,0:T(8,128)}, u32[]{:S(2)}) copy-start(f32[1024,128]{1,0:T(8,128)} %refs_5_.1) | copy-start | bytes 1572868
  3.8 78.4 %copy-start.4 = (f32[1024,128]{1,0:T(8,128)S(1)}, f32[1024,128]{1,0:T(8,128)}, u32[]{:S(2)}) copy-start(f32[1024,128]{1,0:T(8,128)} %refs_6_.1) | copy-start | bytes 1572868

commit v5 on v4

--- a/solution.py
+++ b/solution.py
@@ -261,7 +261,7 @@
         pot[e] = v + step
         return carry
 
-    lax.fori_loop(2, 2 * WIDE + ca - 2, second, 0, unroll=2)
+    lax.fori_loop(2, 2 * WIDE + ca - 2, second, 0, unroll=4)
 
     def third(e, carry):
         v, applied = operate(dir_b, e)
@@ -270,7 +270,7 @@
         pot[e] = pot[e] + step
         return carry
 
-    lax.fori_loop(3, 2 * WIDE + ca - 3, third, 0, unroll=2)
+    lax.fori_loop(3, 2 * WIDE + ca - 3, third, 0, unroll=3)
 
     def joule(a, total):
         v, others = around(pot, a + WIDE)
@@ -283,7 +283,7 @@
         potential[a] = v[ROWS : ROWS + cr]
         return total + jnp.sum(result[ROWS : ROWS + cr], axis=0, keepdims=True)
 
-    part[...] = lax.fori_loop(0, ca, joule, jnp.zeros((1, lanes), jnp.float32))
+    part[...] = lax.fori_loop(0, ca, joule, jnp.zeros((1, lanes), jnp.float32), unroll=2)
     sums[me] = part[...]
 
     def pow_copy(at, j, slot):
@@ -331,8 +331,8 @@
             heat[pl.ds(wanted[j, c] + 7, 1), :] = arrived[pl.ds(j * cap + c, 1), :]
         return carry
 
-    lax.fori_loop(0, n, land, 0)
-    step = 128
+    lax.fori_loop(0, n, land, 0, unroll=2)
+    step = 256
 
     def solve(b, carry):
         at = pl.ds(pl.multiple_of(b * step, 8), step)

time: 87.8 us -> 86.1 us (0.981)
  Pallas kernels: 82.9 us -> 81.2 us
    pallas_call x1, Pallas kernels: 77.5 us -> 76.5 us  [per_device(): pl.pallas_call(kernel, out_shape=(jax.ShapeDtypeStruct(source.shape, jnp....]
where the time goes in v5:
time: 86.1 us; the launch traced here: 85.9 us
  Pallas kernels  81.2 us (94%)
  local copies, waits for them, and re-layouts  1.87 us (2%)
  other arithmetic  1.02 us (1%)
  matrix products  1 us (1%)
    pallas_call x1, Pallas kernels, per_device(): pl.pallas_call(kernel, out_shape=(jax.ShapeDtypeStruct(source.shape, jnp....  76.5 us
    pallas_call x1, Pallas kernels, per_device(): pl.pallas_call(heat_step, out_shape=(jax.ShapeDtypeStruct(temp_old.shape,...  4.72 us

profile of v5, /device:TPU:1, one launch (start us, length us, event | category | flops | bytes accessed | tf_op | source)
XLA Modules:
  0.0 85.9 jit_solution(9441970455632639543)
XLA Ops:
  0.6 0.0 copy-start.5
  0.6 0.0 copy-start.6
  0.6 0.8 eq.28
  1.5 0.5 fusion.2
  2.0 0.1 convert_element_type.63
  2.1 0.0 copy-done.5
  2.1 0.0 copy-done.6
  2.1 0.1 convert_element_type.57
  2.2 0.1 convert_element_type.59
  2.3 1.0 %select_convert_fusion.3 = (bf16[1024,64]{1,0:T(8,128)(2,1)S(1)}, bf16[1024,64]{1,0:T(8,128)(2,1)S(1)}, bf16[1024,64]{1,0:T(8,128)(2,1)S(1)}, bf16[1024,64]{1,0:T(8,128)(2,1)S(1)}) fusion(bf16[1024]{0:T(1024)(128)(2,1)S(1)} %convert_element_type.57, s32[1024]{0:T(1024)S(1)} %convert_element_type.55, bf16[1024]{0:T(1024)(128)(2,1)S(1)} %get-tuple-element.24, ...), kind=kLoop, calls=%fused_computation.15 | loop fusion | flops 327680 | bytes 536576 | tf_op jit(solution)/shard_map/convert
  3.3 0.0 copy-start
  3.3 0.0 copy-start.1
  3.3 0.0 copy-start.2
  3.3 0.5 convolution_convert_fusion
  3.8 0.0 copy-start.3
  3.8 0.0 copy-start.4
  3.8 0.1 reshape.56
  4.0 0.3 copy-done
  4.3 0.2 copy-done.1
  4.5 0.2 copy-done.2
  4.7 76.5 %shard_map.86 = (f32[16,64,128]{2,1,0:T(8,128)S(1)}, f32[2048,128]{1,0:T(8,128)S(1)}, s32[32,1,128]{2,1,0:T(1,128)S(1)}, f32[32,1,128]{2,1,0:T(1,128)S(1)}) custom-call(f32[16,64,128]{2,1,0:T(8,128)S(1)} %copy-done.1, f32[16,64,128]{2,1,0:T(8,128)S(1)} %copy-done.2, f32[1024,128]{1,0:T(8,128)S(1)} %copy-done, s32[32,1,128]{2,1,0:T(1,128)S(1)} %bitcast.14, ...), custom_call_target="tpu_custom_call" | custom-call | tf_op jit(solution)/shard_map/pallas_call | solution.py:376
  81.2 0.0 copy-done.3
  81.2 0.0 copy-done.4
  81.2 4.7 %shard_map.87 = (f32[1024,128]{1,0:T(8,128)}, f32[16,64,128]{2,1,0:T(8,128)}) custom-call(s32[32,64]{1,0:T(8,128)S(1)} %slice_bitcast_fusion.refs_0_, f32[16,64,128]{2,1,0:T(8,128)S(1)} %get-tuple-element.9.refs_1_, f32[2048,128]{1,0:T(8,128)S(1)} %get-tuple-element.10.refs_2_, f32[32,1,128]{2,1,0:T(1,128)S(1)} %get-tuple-element.11.refs_3_, ...), custom_call_target="tpu_custom_call" | custom-call | tf_op jit(solution)/shard_map/pallas_call | solution.py:408
  (9 shorter events, 0.1 us)
Async XLA Ops:
  0.6 1.5 %copy-start.5 = (s32[16,64]{1,0:T(8,128)S(1)}, s32[16,64]{1,0:T(8,128)}, u32[]{:S(2)}) copy-start(s32[16,64]{1,0:T(8,128)} %param.9) | copy-start | bytes 12292
  0.6 1.5 %copy-start.6 = (s32[16,64]{1,0:T(8,128)S(1)}, s32[16,64]{1,0:T(8,128)}, u32[]{:S(2)}) copy-start(s32[16,64]{1,0:T(8,128)} %param.10) | copy-start | bytes 12292
  3.3 1.0 %copy-start = (f32[1024,128]{1,0:T(8,128)S(1)}, f32[1024,128]{1,0:T(8,128)}, u32[]{:S(2)}) copy-start(f32[1024,128]{1,0:T(8,128)} %refs_4_.1) | copy-start | bytes 1572868
  3.3 1.2 %copy-start.1 = (f32[16,64,128]{2,1,0:T(8,128)S(1)}, f32[16,64,128]{2,1,0:T(8,128)}, u32[]{:S(2)}) copy-start(f32[16,64,128]{2,1,0:T(8,128)} %refs_0_.1) | copy-start | bytes 1572868
  3.3 1.3 %copy-start.2 = (f32[16,64,128]{2,1,0:T(8,128)S(1)}, f32[16,64,128]{2,1,0:T(8,128)}, u32[]{:S(2)}) copy-start(f32[16,64,128]{2,1,0:T(8,128)} %refs_1_.1) | copy-start | bytes 1572868
  3.8 77.4 %copy-start.3 = (f32[1024,128]{1,0:T(8,128)S(1)}, f32[1024,128]{1,0:T(8,128)}, u32[]{:S(2)}) copy-start(f32[1024,128]{1,0:T(8,128)} %refs_5_.1) | copy-start | bytes 1572868
  3.8 77.4 %copy-start.4 = (f32[1024,128]{1,0:T(8,128)S(1)}, f32[1024,128]{1,0:T(8,128)}, u32[]{:S(2)}) copy-start(f32[1024,128]{1,0:T(8,128)} %refs_6_.1) | copy-start | bytes 1572868
